TPU v7x, 32 devices: a whole 2x2x4 slice. The times are simulated.
32 devices in a mesh: px: 8 (over y, x, core), py: 4 (over z).
Axes of the slice: x: 2, y: 2, z: 4, core: 2. Of those that a mesh axis runs over, the one named last changes fastest.
Arguments:
- velocity: float32 [8, 1024, 1024], P(None, 'px', 'py'), may hold values from -6 to 6
- forcing: bfloat16 [8, 1024, 1024], P(None, 'px', 'py'), may hold values from -6 to 6
- cross_x: bfloat16 [8, 1024, 1024], P(None, 'px', 'py'), may hold values from -1.5 to 1.5
- cross_y: bfloat16 [8, 1024, 1024], P(None, 'px', 'py'), may hold values from -1.5 to 1.5
- inv_x: bfloat16 [8, 1024, 1024], P('px'), may hold values from -1 to 2, as said below
- inv_y: bfloat16 [8, 1024, 1024], P('px'), may hold values from -1 to 2, as said below
Outputs:
- velocity_new: float32 [8, 1024, 1024], P(None, 'px', 'py')
Inputs may be any that keep to these rules, and one draw needn't show every extreme that they name: `inv_x`: a dense matrix for each level. `inv_y`: a dense matrix for each level.
All inputs are finite; a program needn't handle non-finite values.
Results may differ from a plain program's by a relative error of at most 0.0052.
Values may be sent and summed in bfloat16 or wider, within the bound.
A program may use at most 64 MiB of HBM per device.

v0:
```python
import functools

import jax
import jax.numpy as jnp
from jax import lax
from jax.experimental import pallas as pl
from jax.experimental.pallas import tpu as pltpu
from jax.sharding import PartitionSpec as P

time_step = 0.25


def with_halo(cells, sides, width):
    for axis, dim in sides:
        count = lax.axis_size(axis)
        head = lax.slice_in_dim(cells, 0, width, axis=dim)
        tail = lax.slice_in_dim(cells, cells.shape[dim] - width, cells.shape[dim], axis=dim)
        cells = jnp.concatenate(
            [
                lax.ppermute(tail, axis, [(i, (i + 1) % count) for i in range(count)]),
                cells,
                lax.ppermute(head, axis, [((i + 1) % count, i) for i in range(count)]),
            ],
            axis=dim,
        )
    return cells


def shards(velocity, forcing, cross_x, cross_y, inv_x, inv_y):
    padded = with_halo(velocity, (("px", 1), ("py", 2)), 1)
    x_plus = padded[:, 2:, 1:-1]
    x_minus = padded[:, :-2, 1:-1]
    y_plus = padded[:, 1:-1, 2:]
    y_minus = padded[:, 1:-1, :-2]
    z_padded = jnp.pad(velocity, ((1, 1), (0, 0), (0, 0)))
    laplace = (
        x_plus
        + x_minus
        + y_plus
        + y_minus
        - 4.0 * velocity
        + z_padded[2:]
        + z_padded[:-2]
        - 2.0 * velocity
    )
    slope_x = jnp.pad(0.5 * (x_plus - x_minus), ((1, 1), (0, 0), (0, 0)))
    slope_y = jnp.pad(0.5 * (y_plus - y_minus), ((1, 1), (0, 0), (0, 0)))
    mixed_x = 0.5 * (slope_x[2:] - slope_x[:-2])
    mixed_y = 0.5 * (slope_y[2:] - slope_y[:-2])
    total = (
        laplace
        + cross_x.astype(jnp.float32) * mixed_x
        + cross_y.astype(jnp.float32) * mixed_y
        + forcing.astype(jnp.float32)
    )
    rhs = (time_step * total).astype(jnp.bfloat16)
    section_one = jnp.einsum(
        "lab,lbk->lak",
        inv_x,
        lax.all_to_all(rhs, "px", split_axis=0, concat_axis=1, tiled=True),
        preferred_element_type=jnp.float32,
    ).astype(jnp.bfloat16)
    y_lines = lax.all_to_all(section_one, "py", split_axis=1, concat_axis=2, tiled=True)
    section_two = jnp.einsum("lxb,lab->lxa", y_lines, inv_y, preferred_element_type=jnp.float32)
    settled = lax.all_to_all(
        lax.all_to_all(section_two, "py", split_axis=2, concat_axis=1, tiled=True),
        "px",
        split_axis=1,
        concat_axis=0,
        tiled=True,
    )
    return velocity + settled


def send(src, dst, send_sem, recv_sem, target):
    return pltpu.make_async_remote_copy(
        src_ref=src,
        dst_ref=dst,
        send_sem=send_sem,
        recv_sem=recv_sem,
        device_id=target,
        device_id_type=pl.DeviceIdType.MESH,
    )


def kernel(
    npx,
    npy,
    vel_hbm,
    frc_hbm,
    cx_hbm,
    cy_hbm,
    ix_hbm,
    iy_hbm,
    out,
    vel,
    frc,
    cx,
    cy,
    ix,
    iy,
    x_low,
    x_high,
    y_send,
    y_recv,
    slope_x,
    slope_y,
    lap,
    rhs,
    lines_x,
    one,
    lines_y,
    two,
    load_sem,
    halo_send,
    halo_recv,
    rhs_send,
    rhs_recv,
    one_send,
    one_recv,
    two_send,
    out_recv,
):
    me = lax.axis_index("px")
    my = lax.axis_index("py")
    levels, rows, cols = vel.shape
    part = rows // npy
    chunks = rhs.shape[0]
    wide = cols // chunks
    pieces = [(vel_hbm, vel), (frc_hbm, frc), (cx_hbm, cx), (cy_hbm, cy), (ix_hbm, ix), (iy_hbm, iy)]
    loads = [pltpu.make_async_copy(a, b, load_sem.at[i]) for i, (a, b) in enumerate(pieces)]
    loads[0].start()

    barrier = pltpu.get_barrier_semaphore()
    for step in range(1, npx):
        pl.semaphore_signal(barrier, inc=1, device_id={"px": lax.rem(me + step, npx)}, device_id_type=pl.DeviceIdType.MESH)
    for step in range(1, npy):
        pl.semaphore_signal(barrier, inc=1, device_id={"py": lax.rem(my + step, npy)}, device_id_type=pl.DeviceIdType.MESH)

    loads[0].wait()
    for load in loads[1:]:
        load.start()
    lane = lax.broadcasted_iota(jnp.int32, (rows, 128), 1)

    def gather_face(level, faces):
        first, last = faces
        now = vel[level]
        first = jnp.where(lane == level, now[:, 0:1], first)
        last = jnp.where(lane == level, now[:, cols - 1 : cols], last)
        return first, last

    zero = jnp.zeros((rows, 128), jnp.float32)
    first, last = lax.fori_loop(0, levels, gather_face, (zero, zero))
    y_send[0] = jnp.transpose(first)[:levels]
    y_send[1] = jnp.transpose(last)[:levels]
    pl.semaphore_wait(barrier, npx + npy - 2)

    up_x, down_x = lax.rem(me + 1, npx), lax.rem(me + npx - 1, npx)
    up_y, down_y = lax.rem(my + 1, npy), lax.rem(my + npy - 1, npy)
    halos = [
        send(y_send.at[1], y_recv.at[0], halo_send.at[0], halo_recv.at[0], {"py": up_y}),
        send(y_send.at[0], y_recv.at[1], halo_send.at[1], halo_recv.at[1], {"py": down_y}),
        send(vel.at[:, pl.ds(rows - 8, 8), :], x_low, halo_send.at[2], halo_recv.at[2], {"px": up_x}),
        send(vel.at[:, pl.ds(0, 8), :], x_high, halo_send.at[3], halo_recv.at[3], {"px": down_x}),
    ]
    for halo in halos:
        halo.start()
    row_at = lax.broadcasted_iota(jnp.int32, (rows, cols), 0)
    col_at = lax.broadcasted_iota(jnp.int32, (rows, cols), 1)
    blank = jnp.zeros((rows, cols), jnp.float32)
    for edge in (0, levels + 1):
        slope_x[edge] = blank
        slope_y[edge] = blank

    def slopes(level, _):
        now = vel[level]
        x_minus = jnp.where(row_at == 0, 0.0, pltpu.roll(now, 1, 0))
        x_plus = jnp.where(row_at == rows - 1, 0.0, pltpu.roll(now, rows - 1, 0))
        y_minus = jnp.where(col_at == 0, 0.0, pltpu.roll(now, 1, 1))
        y_plus = jnp.where(col_at == cols - 1, 0.0, pltpu.roll(now, cols - 1, 1))
        slope_x[level + 1] = 0.5 * (x_plus - x_minus)
        slope_y[level + 1] = 0.5 * (y_plus - y_minus)
        lap[level] = x_plus + x_minus + y_plus + y_minus - 4.0 * now
        return 0

    lax.fori_loop(0, levels, slopes, 0)
    for load in loads[1:4]:
        load.wait()

    def inner(level, _):
        above = jnp.minimum(level + 1, levels - 1)
        below = jnp.maximum(level - 1, 0)
        z_plus = jnp.where(level < levels - 1, 1.0, 0.0) * vel[above]
        z_minus = jnp.where(level > 0, 1.0, 0.0) * vel[below]
        total = lap[level] + z_plus + z_minus - 2.0 * vel[level]
        total += cx[level].astype(jnp.float32) * (0.5 * (slope_x[level + 2] - slope_x[level]))
        total += cy[level].astype(jnp.float32) * (0.5 * (slope_y[level + 2] - slope_y[level]))
        lap[level] = total + frc[level].astype(jnp.float32)
        return 0

    lax.fori_loop(0, levels, inner, 0)
    for halo in halos:
        halo.wait_recv()

    def level_slope(face, axis, at):
        size = face.shape[axis]
        lower = jnp.where(at == 0, 0.0, pltpu.roll(face, 1, axis))
        upper = jnp.where(at == levels - 1, 0.0, pltpu.roll(face, size - 1, axis))
        return 0.25 * (upper - lower)

    spare = jnp.zeros((128 - levels, rows), jnp.float32)
    face_low = jnp.transpose(jnp.concatenate([y_recv[0], spare], axis=0))
    face_high = jnp.transpose(jnp.concatenate([y_recv[1], spare], axis=0))
    mixed_low = -level_slope(face_low, 1, lane)
    mixed_high = level_slope(face_high, 1, lane)
    level_at = lax.broadcasted_iota(jnp.int32, (levels, cols), 0)
    x_face = (x_low[:, 7, :], x_high[:, 0, :])
    x_mixed = (-level_slope(x_face[0], 0, level_at), level_slope(x_face[1], 0, level_at))
    slab_at = lax.broadcasted_iota(jnp.int32, (16, wide), 0)
    wide_at = lax.broadcasted_iota(jnp.int32, (rows, wide), 1)

    def right_side(chunk, at):
        level = lax.rem(me + 1 + at, npx)
        side = slice(chunk * wide, (chunk + 1) * wide)

        def row(faces):
            return jnp.sum(jnp.where(level_at[:, side] == level, faces, 0.0), axis=0, keepdims=True)

        for end, first in enumerate((0, rows - 16)):
            slab = slice(first, first + 16)
            face = row(x_face[end][:, side]) + cx[level, slab, side].astype(jnp.float32) * row(x_mixed[end][:, side])
            lap[level, slab, side] += jnp.where(slab_at == 15 * end, face, 0.0)
        total = lap[level, :, side]

        def column(faces):
            return jnp.sum(jnp.where(lane == level, faces, 0.0), axis=1, keepdims=True)

        for at_chunk, at_col, faces, mixed in ((0, 0, face_low, mixed_low), (chunks - 1, wide - 1, face_high, mixed_high)):
            if chunk == at_chunk:
                face = column(faces) + cy[level, :, side].astype(jnp.float32) * column(mixed)
                total += jnp.where(wide_at == at_col, face, 0.0)
        value = (time_step * total).astype(jnp.bfloat16)

        @pl.when(at < npx - 1)
        def _():
            rhs[chunk, level] = value
            to_px(chunk, level).start()

        @pl.when(at == npx - 1)
        def _():
            lines_x[chunk, me] = value

    def to_px(chunk, other):
        return send(
            rhs.at[chunk, other], lines_x.at[chunk, me], rhs_send.at[chunk, other], rhs_recv.at[chunk, me], {"px": other}
        )

    def from_px(chunk, other):
        return send(
            rhs.at[chunk, other], lines_x.at[chunk, other], rhs_send.at[chunk, other], rhs_recv.at[chunk, other], {"px": other}
        )

    def over_px(body):
        def one_step(at, _):
            body(lax.rem(me + at, npx))
            return 0

        lax.fori_loop(1, npx, one_step, 0)

    for chunk in range(chunks):
        def one_level(at, _):
            right_side(chunk, at)
            return 0

        lax.fori_loop(0, npx, one_level, 0)

    half = part // 2
    forward = [(chunk, 0, part) for chunk in range(chunks - 1)] + [(chunks - 1, 0, half), (chunks - 1, half, half)]
    order = [*range(1, npy), 0]
    turn = jnp.where(my < npy // 2, 1, npy - 1)

    def mate(step):
        return lax.rem(my + step * turn, npy)

    order_x, order_y = npx * rows, npy * cols

    def strip(at, chunk=0, width=cols):
        return pl.ds(pl.multiple_of(at * cols + chunk * wide, wide), width)

    def piece_y(index, other, source):
        chunk, first, count = forward[index]
        return send(
            one.at[index, other, :, pl.ds(0, count)],
            lines_y.at[:, pl.ds(first, count), strip(source, chunk, wide)],
            one_send.at[index, other],
            one_recv.at[index, source],
            {"py": other},
        )

    loads[4].wait()
    for index, (chunk, first, count) in enumerate(forward):
        if first == 0:
            over_px(lambda other: from_px(chunk, other).wait_recv())
        for step in order:
            other = mate(step)
            mine = ix[:, pl.ds(pl.multiple_of(other * part + first, half), count), :].reshape(npx * count, order_x)
            value = jnp.dot(mine, lines_x[chunk].reshape(order_x, wide), preferred_element_type=jnp.float32)
            value = value.astype(jnp.bfloat16).reshape(npx, count, wide)
            if step:
                one[index, other, :, 0:count] = value
                piece_y(index, other, my).start()
            else:
                lines_y[:, first : first + count, strip(my, chunk, wide)] = value

    def cut(side, origin):
        return pl.ds(pl.multiple_of(origin * part + side * half, half), half)

    def to_cells(side, other_y, other_x):
        return send(
            two.at[side, other_y, other_x],
            out.at[me, cut(side, my), :],
            two_send.at[side, other_y, other_x],
            out_recv.at[me],
            {"px": other_x, "py": other_y},
        )

    def own(side):
        return pltpu.make_async_copy(two.at[side, my, me], out.at[me, cut(side, my), :], out_recv.at[me])

    loads[5].wait()
    for side in range(2):
        for index, (chunk, first, count) in enumerate(forward):
            if first == side * half:
                for step in range(1, npy):
                    source = lax.rem(my + step, npy)
                    piece_y(index, source, source).wait_recv()
        held = lines_y[:, side * half : (side + 1) * half, :].reshape(npx * half, order_y)
        for step in order:
            other = mate(step)
            value = lax.dot_general(held, iy[strip(other), :], (((1,), (1,)), ((), ())), preferred_element_type=jnp.float32)
            two[side, other] = value.astype(jnp.bfloat16).reshape(npx, half, cols)
            over_px(lambda other_x: to_cells(side, other, other_x).start())
            if step:
                to_cells(side, other, me).start()
            else:
                own(side).start()

    def settle(other):
        send(out.at[other], out.at[other], rhs_send.at[0, other], out_recv.at[other], {"px": other}).wait_recv()
        for chunk in range(chunks):
            to_px(chunk, other).wait_send()

    over_px(settle)
    pltpu.make_async_copy(out.at[me], out.at[me], out_recv.at[me]).wait()
    for halo in halos:
        halo.wait_send()
    for step in range(1, npy):
        other = lax.rem(my + step, npy)
        for index in range(len(forward)):
            piece_y(index, other, my).wait_send()
    for side in range(2):
        for step in range(npy):
            other = lax.rem(my + step, npy)
            over_px(lambda other_x: to_cells(side, other, other_x).wait_send())
            if step:
                to_cells(side, other, me).wait_send()


def fused(velocity, forcing, cross_x, cross_y, inv_x, inv_y):
    npx, npy = lax.axis_size("px"), lax.axis_size("py")
    levels, rows, cols = velocity.shape
    part = rows // npy
    half, chunks = part // 2, cols // 128
    wide = cols // chunks
    shape, narrow = velocity.shape, jnp.bfloat16
    order_x, order_y = npx * rows, npy * cols
    vmem, dma = pltpu.VMEM, pltpu.SemaphoreType.DMA
    settled = pl.pallas_call(
        functools.partial(kernel, npx, npy),
        out_shape=jax.ShapeDtypeStruct(shape, narrow),
        in_specs=[pl.BlockSpec(memory_space=pl.ANY)] * 6,
        out_specs=pl.BlockSpec(memory_space=pl.ANY),
        scratch_shapes=[
            vmem(shape, jnp.float32),
            vmem(shape, narrow),
            vmem(shape, narrow),
            vmem(shape, narrow),
            vmem((npx, rows, order_x), narrow),
            vmem((order_y, order_y), narrow),
            vmem((levels, 8, cols), jnp.float32),
            vmem((levels, 8, cols), jnp.float32),
            vmem((2, levels, rows), jnp.float32),
            vmem((2, levels, rows), jnp.float32),
            vmem((levels + 2, rows, cols), jnp.float32),
            vmem((levels + 2, rows, cols), jnp.float32),
            vmem(shape, jnp.float32),
            vmem((chunks, levels, rows, wide), narrow),
            vmem((chunks, npx, rows, wide), narrow),
            vmem((chunks + 1, npy, npx, part, wide), narrow),
            vmem((npx, part, order_y), narrow),
            vmem((2, npy, npx, half, cols), narrow),
            dma((6,)),
            dma((4,)),
            dma((4,)),
            dma((chunks, npx)),
            dma((chunks, npx)),
            dma((chunks + 1, npy)),
            dma((chunks + 1, npy)),
            dma((2, npy, npx)),
            dma((npx,)),
        ],
        compiler_params=pltpu.CompilerParams(collective_id=0, has_side_effects=True, vmem_limit_bytes=56_000_000),
        cost_estimate=pl.CostEstimate(flops=4 * order_x * order_y * rows, bytes_accessed=8 * 1024 * 1024, transcendentals=0),
    )(
        velocity,
        forcing,
        cross_x,
        cross_y,
        inv_x.reshape(npx, rows, order_x),
        inv_y.reshape(order_y, order_y),
    )
    return velocity + settled.astype(jnp.float32)


def step(velocity, forcing, cross_x, cross_y, inv_x, inv_y):
    npx, npy = lax.axis_size("px"), lax.axis_size("py")
    levels, rows, cols = velocity.shape
    aligned = rows % (32 * npy) == 0 and rows % 128 == 0 and cols % 128 == 0 and levels % 8 == 0
    if aligned and levels == npx and levels <= 128 and inv_x.shape[0] == 1:
        return fused(velocity, forcing, cross_x, cross_y, inv_x, inv_y)
    return shards(velocity, forcing, cross_x, cross_y, inv_x, inv_y)


def solution(mesh):
    return jax.shard_map(
        step,
        mesh=mesh,
        in_specs=(
            P(None, "px", "py"),
            P(None, "px", "py"),
            P(None, "px", "py"),
            P(None, "px", "py"),
            P("px", None, None),
            P("px", None, None),
        ),
        out_specs=P(None, "px", "py"),
        check_vma=False,
    )
```

profile of v0, /device:TPU:0, one launch (start us, length us, event | category | flops | bytes accessed | tf_op | source)
XLA Modules:
  0.0 43.3 jit_solution(16214635934914355547)
XLA Ops:
  0.0 0.0 copy-start
  0.0 42.2 %shard_map.64 = bf16[8,128,256]{2,1,0:T(8,128)(2,1)S(1)} custom-call(f32[8,128,256]{2,1,0:T(8,128)} %vel_hbm.1, bf16[8,128,256]{2,1,0:T(8,128)(2,1)} %frc_hbm.1, bf16[8,128,256]{2,1,0:T(8,128)(2,1)} %cx_hbm.1, bf16[8,128,256]{2,1,0:T(8,128)(2,1)} %cy_hbm.1, bf16[8,128,1024]{2,1,0:T(8,128)(2,1)} %bitcast.2, bf16[1024,1024]{1,0:T(8,128)(2,1)} %bitcast.3), custom_call_target="tpu_custom_call" | custom-call | flops 536870912 | bytes 8388608 | tf_op jit(solution)/shard_map/pallas_call | solution.py:378
  42.2 0.0 copy-done
  42.2 1.1 %convert_add_fusion = f32[8,128,256]{2,1,0:T(8,128)} fusion(f32[8,128,256]{2,1,0:T(8,128)S(1)} %copy-done, bf16[8,128,256]{2,1,0:T(8,128)(2,1)S(1)} %shard_map.64), kind=kLoop, calls=%fused_computation | loop fusion | flops 524288 | bytes 2621440 | tf_op jit(solution)/shard_map/add | solution.py:422
Async XLA Ops:
  0.0 42.2 %copy-start = (f32[8,128,256]{2,1,0:T(8,128)S(1)}, f32[8,128,256]{2,1,0:T(8,128)}, u32[]{:S(2)}) copy-start(f32[8,128,256]{2,1,0:T(8,128)} %vel_hbm.1) | copy-start | bytes 3145732
where the time goes:
time: 43.4 us; the launch traced here: 43.3 us
  Pallas kernels  42.2 us (97%)
  other arithmetic  1.09 us (3%)
    pallas_call x1, Pallas kernels, fused(): pl.pallas_call(functools.partial(kernel, npx, npy), out_shape=jax.ShapeDt...  42.2 us
    add x1, other arithmetic, fused(): return velocity + settled.astype(jnp.float32)  1.09 us

commit v1 on v0

v1 whole, which is shorter than its diff:
```python
import functools

import jax
import jax.numpy as jnp
from jax import lax
from jax.experimental import pallas as pl
from jax.experimental.pallas import tpu as pltpu
from jax.sharding import PartitionSpec as P

time_step = 0.25


def with_halo(cells, sides, width):
    for axis, dim in sides:
        count = lax.axis_size(axis)
        head = lax.slice_in_dim(cells, 0, width, axis=dim)
        tail = lax.slice_in_dim(cells, cells.shape[dim] - width, cells.shape[dim], axis=dim)
        cells = jnp.concatenate(
            [
                lax.ppermute(tail, axis, [(i, (i + 1) % count) for i in range(count)]),
                cells,
                lax.ppermute(head, axis, [((i + 1) % count, i) for i in range(count)]),
            ],
            axis=dim,
        )
    return cells


def shards(velocity, forcing, cross_x, cross_y, inv_x, inv_y):
    padded = with_halo(velocity, (("px", 1), ("py", 2)), 1)
    x_plus = padded[:, 2:, 1:-1]
    x_minus = padded[:, :-2, 1:-1]
    y_plus = padded[:, 1:-1, 2:]
    y_minus = padded[:, 1:-1, :-2]
    z_padded = jnp.pad(velocity, ((1, 1), (0, 0), (0, 0)))
    laplace = (
        x_plus
        + x_minus
        + y_plus
        + y_minus
        - 4.0 * velocity
        + z_padded[2:]
        + z_padded[:-2]
        - 2.0 * velocity
    )
    slope_x = jnp.pad(0.5 * (x_plus - x_minus), ((1, 1), (0, 0), (0, 0)))
    slope_y = jnp.pad(0.5 * (y_plus - y_minus), ((1, 1), (0, 0), (0, 0)))
    mixed_x = 0.5 * (slope_x[2:] - slope_x[:-2])
    mixed_y = 0.5 * (slope_y[2:] - slope_y[:-2])
    total = (
        laplace
        + cross_x.astype(jnp.float32) * mixed_x
        + cross_y.astype(jnp.float32) * mixed_y
        + forcing.astype(jnp.float32)
    )
    rhs = (time_step * total).astype(jnp.bfloat16)
    section_one = jnp.einsum(
        "lab,lbk->lak",
        inv_x,
        lax.all_to_all(rhs, "px", split_axis=0, concat_axis=1, tiled=True),
        preferred_element_type=jnp.float32,
    ).astype(jnp.bfloat16)
    y_lines = lax.all_to_all(section_one, "py", split_axis=1, concat_axis=2, tiled=True)
    section_two = jnp.einsum("lxb,lab->lxa", y_lines, inv_y, preferred_element_type=jnp.float32)
    settled = lax.all_to_all(
        lax.all_to_all(section_two, "py", split_axis=2, concat_axis=1, tiled=True),
        "px",
        split_axis=1,
        concat_axis=0,
        tiled=True,
    )
    return velocity + settled


def send(src, dst, send_sem, recv_sem, target):
    return pltpu.make_async_remote_copy(
        src_ref=src,
        dst_ref=dst,
        send_sem=send_sem,
        recv_sem=recv_sem,
        device_id=target,
        device_id_type=pl.DeviceIdType.MESH,
    )


def kernel(
    npx,
    npy,
    vel_hbm,
    frc_hbm,
    cx_hbm,
    cy_hbm,
    ix_hbm,
    iy_hbm,
    out,
    vel,
    frc,
    cx,
    cy,
    ix,
    iy,
    x_send,
    x_recv,
    x_mixed,
    y_send,
    y_recv,
    slope_x,
    slope_y,
    lap,
    rhs,
    lines,
    cross,
    mid,
    two,
    fin,
    fix_send,
    fix_recv,
    fix_rows,
    fix_cols,
    load_sem,
    halo_send,
    halo_recv,
    rhs_send,
    own_send,
    fix_sent,
    fix_own,
    fix_come,
    lines_come,
    cross_come,
    mid_send,
    two_send,
    two_own,
    fin_send,
    out_recv,
):
    me = lax.axis_index("px")
    my = lax.axis_index("py")
    levels, rows, cols = vel.shape
    part = rows // npy
    order_x, order_y = npx * rows, npy * cols
    x_first = lax.rem(me, 2) == 0
    pieces = [(vel_hbm, vel), (frc_hbm, frc), (cx_hbm, cx), (cy_hbm, cy), (ix_hbm, ix), (iy_hbm, iy)]
    loads = [pltpu.make_async_copy(a, b, load_sem.at[i]) for i, (a, b) in enumerate(pieces)]
    loads[0].start()

    barrier = pltpu.get_barrier_semaphore()

    def greet(at, _):
        other = lax.rem(me * npy + my + at, npx * npy)
        pl.semaphore_signal(
            barrier, inc=1, device_id={"px": other // npy, "py": lax.rem(other, npy)}, device_id_type=pl.DeviceIdType.MESH
        )
        return 0

    lax.fori_loop(1, npx * npy, greet, 0)
    fix_rows[...] = jnp.zeros_like(fix_rows)
    loads[0].wait()
    for load in loads[1:]:
        load.start()
    lane = lax.broadcasted_iota(jnp.int32, (rows, 128), 1)
    zero = jnp.zeros((rows, 128), jnp.float32)

    def ends_of(ref):
        def one_level(level, faces):
            first, last = faces
            first = jnp.where(lane == level, ref[level, :, 0:1].astype(jnp.float32), first)
            last = jnp.where(lane == level, ref[level, :, cols - 1 : cols].astype(jnp.float32), last)
            return first, last

        first, last = lax.fori_loop(0, levels, one_level, (zero, zero))
        return jnp.transpose(first)[:levels], jnp.transpose(last)[:levels]

    y_send[0], y_send[1] = ends_of(vel)
    for level in range(levels):
        x_send[0, level : level + 1, :] = vel[level, 0:1, :]
        x_send[1, level : level + 1, :] = vel[level, rows - 1 : rows, :]
    pl.semaphore_wait(barrier, npx * npy - 1)

    up_x, down_x = lax.rem(me + 1, npx), lax.rem(me + npx - 1, npx)
    up_y, down_y = lax.rem(my + 1, npy), lax.rem(my + npy - 1, npy)
    halos_y = [
        send(y_send.at[1], y_recv.at[0], halo_send.at[0], halo_recv.at[0], {"py": up_y}),
        send(y_send.at[0], y_recv.at[1], halo_send.at[1], halo_recv.at[1], {"py": down_y}),
    ]
    halos_x = [
        send(x_send.at[1], x_recv.at[0], halo_send.at[2], halo_recv.at[2], {"px": up_x}),
        send(x_send.at[0], x_recv.at[1], halo_send.at[3], halo_recv.at[3], {"px": down_x}),
    ]
    for halo in halos_y + halos_x:
        halo.start()
    row_at = lax.broadcasted_iota(jnp.int32, (rows, cols), 0)
    col_at = lax.broadcasted_iota(jnp.int32, (rows, cols), 1)
    blank = jnp.zeros((rows, cols), jnp.float32)
    for edge in (0, levels + 1):
        slope_x[edge] = blank
        slope_y[edge] = blank

    def slopes(level, _):
        now = vel[level]
        x_minus = jnp.where(row_at == 0, 0.0, pltpu.roll(now, 1, 0))
        x_plus = jnp.where(row_at == rows - 1, 0.0, pltpu.roll(now, rows - 1, 0))
        y_minus = jnp.where(col_at == 0, 0.0, pltpu.roll(now, 1, 1))
        y_plus = jnp.where(col_at == cols - 1, 0.0, pltpu.roll(now, cols - 1, 1))
        slope_x[level + 1] = 0.5 * (x_plus - x_minus)
        slope_y[level + 1] = 0.5 * (y_plus - y_minus)
        lap[level] = x_plus + x_minus + y_plus + y_minus - 4.0 * now
        return 0

    lax.fori_loop(0, levels, slopes, 0)
    for load in loads[1:4]:
        load.wait()

    def strip(at):
        return pl.ds(pl.multiple_of(at * cols, cols), cols)

    def rows_of(at):
        return pl.ds(pl.multiple_of(at * part, part), part)

    def inner(level):
        above = jnp.minimum(level + 1, levels - 1)
        below = jnp.maximum(level - 1, 0)
        z_plus = jnp.where(level < levels - 1, 1.0, 0.0) * vel[above]
        z_minus = jnp.where(level > 0, 1.0, 0.0) * vel[below]
        total = lap[level] + z_plus + z_minus - 2.0 * vel[level]
        total += cx[level].astype(jnp.float32) * (0.5 * (slope_x[level + 2] - slope_x[level]))
        total += cy[level].astype(jnp.float32) * (0.5 * (slope_y[level + 2] - slope_y[level]))
        total += frc[level].astype(jnp.float32)
        lap[level] = total
        rhs[level] = (time_step * total).astype(jnp.bfloat16)

    def to_cross(level, other):
        src, dst = rhs.at[level, rows_of(other), :], cross.at[me, :, strip(my)]

        def away(sem):
            return send(src, dst, sem, cross_come, {"px": level, "py": other})

        @pl.when(level != me)
        def _():
            away(rhs_send.at[level]).start()

        @pl.when((level == me) & (other != my))
        def _():
            away(own_send.at[other]).start()

        @pl.when((level == me) & (other == my))
        def _():
            pltpu.make_async_copy(src, dst, cross_come).start()

    def to_lines(level):
        @pl.when(level != me)
        def _():
            send(rhs.at[level], lines.at[me], rhs_send.at[level], lines_come, {"px": level}).start()

        @pl.when(level == me)
        def _():
            pltpu.make_async_copy(rhs.at[level], lines.at[me], lines_come).start()

    pairs = npx // 2

    def level_of(at, odd):
        return 2 * lax.rem(me // 2 + 1 + at, pairs) + odd

    def early(at, _):
        level = level_of(at, 1)
        inner(level)
        for other in range(1, npy - 1):
            to_cross(level, other)
        return 0

    def early_even(at, _):
        inner(level_of(at, 0))
        return 0

    lax.fori_loop(0, pairs, early, 0)
    lax.fori_loop(0, pairs, early_even, 0)
    for halo in halos_x:
        halo.wait_recv()

    def level_slope(face):
        at = lax.broadcasted_iota(jnp.int32, face.shape, 0)
        lower = jnp.where(at == 0, 0.0, pltpu.roll(face, 1, 0))
        upper = jnp.where(at == levels - 1, 0.0, pltpu.roll(face, levels - 1, 0))
        return 0.25 * (upper - lower)

    x_mixed[0] = -level_slope(x_recv[0])
    x_mixed[1] = level_slope(x_recv[1])
    slab_at = lax.broadcasted_iota(jnp.int32, (16, cols), 0)

    def fix_x(level):
        for end, first in enumerate((0, rows - 16)):
            slab = slice(first, first + 16)
            face = x_recv[end, pl.ds(level, 1), :] + cx[level, slab, :].astype(jnp.float32) * x_mixed[end, pl.ds(level, 1), :]
            total = lap[level, slab, :] + jnp.where(slab_at == 15 * end, face, 0.0)
            lap[level, slab, :] = total
            rhs[level, slab, :] = (time_step * total).astype(jnp.bfloat16)

    def late(at, _):
        level = level_of(at, 1)
        fix_x(level)
        for other in sorted({0, npy - 1}):
            to_cross(level, other)
        return 0

    def late_even(at, _):
        level = level_of(at, 0)
        fix_x(level)
        to_lines(level)
        return 0

    lax.fori_loop(0, pairs, late, 0)
    lax.fori_loop(0, pairs, late_even, 0)

    near, far = ends_of(lap), ends_of(cy)
    for halo in halos_y:
        halo.wait_recv()
    for end in range(2):
        face = y_recv[end]
        mixed = level_slope(face) if end else -level_slope(face)
        value = time_step * (near[end] + face + far[end] * mixed)
        for level in range(levels):
            fix_send[level, end : end + 1, :] = value[level : level + 1, :]

    def fix_to(level, other, sem):
        return send(fix_send.at[level], fix_recv.at[my, me], sem, fix_come, {"px": level, "py": other})

    def give_even(at, _):
        level = level_of(at, 0)

        @pl.when(level != me)
        def _():
            fix_to(level, my, fix_sent.at[level]).start()

        @pl.when(level == me)
        def _():
            pltpu.make_async_copy(fix_send.at[level], fix_recv.at[my, me], fix_come).start()

        return 0

    def give_odd(at, _):
        level = level_of(at, 1)
        for other in range(npy):
            @pl.when(level != me)
            def _():
                fix_to(level, other, fix_sent.at[level]).start()

            @pl.when((level == me) & (other != my))
            def _():
                fix_to(level, other, fix_own.at[other]).start()

            @pl.when((level == me) & (other == my))
            def _():
                pltpu.make_async_copy(fix_send.at[level], fix_recv.at[my, me], fix_come).start()

        return 0

    lax.fori_loop(0, pairs, give_even, 0)
    lax.fori_loop(0, pairs, give_odd, 0)

    order = [*range(1, npy), 0]
    turn = jnp.where(my < npy // 2, 1, npy - 1)

    def mate(step):
        return lax.rem(my + step * turn, npy)

    def whole(ref, sem):
        return pltpu.make_async_copy(ref, ref, sem)

    def narrow(value, shape):
        return value.astype(jnp.bfloat16).reshape(shape)

    def mend(ref, at, where_cols, value):
        for end in range(2):
            first = where_cols + (cols - 128) * end
            now = ref[at, :, first : first + 128].astype(jnp.float32)
            spot = lane[: now.shape[0]] == 127 * end
            ref[at, :, first : first + 128] = jnp.where(spot, value(end), now).astype(jnp.bfloat16)

    def mid_to_cross(other, source):
        return send(mid.at[other], cross.at[:, :, strip(source)], mid_send.at[other], cross_come, {"py": other})

    def mid_to_lines(other, source):
        return send(mid.at[other], lines.at[:, rows_of(source), :], mid_send.at[other], lines_come, {"py": other})

    def two_to(other_y, other_x, sem):
        return send(
            two.at[other_y, other_x], out.at[me, rows_of(my), :], sem, out_recv.at[me], {"px": other_x, "py": other_y}
        )

    def fin_to(other):
        return send(fin.at[other], out.at[me], fin_send.at[other], out_recv.at[me], {"px": other})

    def over_px(body):
        def one_step(at, _):
            body(lax.rem(me + at, npx))
            return 0

        lax.fori_loop(1, npx, one_step, 0)

    @pl.when(x_first)
    def _():
        whole(fix_recv.at[my], fix_come).wait()
        for p in range(npx):
            fix_rows[2 * p : 2 * p + 2, :] = fix_recv[my, p]
        fix_cols[...] = jnp.transpose(fix_rows[...])
        whole(lines, lines_come).wait()
        for p in range(npx):
            mend(lines, p, 0, lambda end: fix_cols[:, 2 * p + end : 2 * p + end + 1])
        loads[4].wait()
        for step in order:
            other = mate(step)
            mine = ix[:, rows_of(other), :].reshape(npx * part, order_x)
            value = jnp.dot(mine, lines[...].reshape(order_x, cols), preferred_element_type=jnp.float32)
            mid[other] = narrow(value, (npx, part, cols))
            if step:
                mid_to_cross(other, my).start()
            else:
                pltpu.make_async_copy(mid.at[my], cross.at[:, :, strip(my)], cross_come).start()
        loads[5].wait()
        whole(cross, cross_come).wait()
        for step in order:
            other = mate(step)
            value = lax.dot_general(
                cross[...].reshape(npx * part, order_y),
                iy[strip(other), :],
                (((1,), (1,)), ((), ())),
                preferred_element_type=jnp.float32,
            )
            two[other] = narrow(value, (npx, part, cols))
            if step:
                over_px(lambda other_x: two_to(other, other_x, two_send.at[other]).start())
                two_to(other, me, two_send.at[other]).start()
            else:
                over_px(lambda other_x: two_to(my, other_x, two_own.at[other_x]).start())
                pltpu.make_async_copy(two.at[my, me], out.at[me, rows_of(my), :], out_recv.at[me]).start()

    @pl.when(jnp.logical_not(x_first))
    def _():
        whole(fix_recv, fix_come).wait()
        for q in range(npy):
            for p in range(npx):
                at = 2 * (q * npx + p)
                fix_rows[at : at + 2, :] = fix_recv[q, p]
        fix_cols[...] = jnp.transpose(fix_rows[...])
        whole(cross, cross_come).wait()
        for q in range(npy):
            for p in range(npx):
                at = 2 * (q * npx + p)
                mend(cross, p, q * cols, lambda end: fix_cols[rows_of(my), at + end : at + end + 1])
        loads[5].wait()
        for step in order:
            other = mate(step)
            value = lax.dot_general(
                cross[...].reshape(npx * part, order_y),
                iy[strip(other), :],
                (((1,), (1,)), ((), ())),
                preferred_element_type=jnp.float32,
            )
            mid[other] = narrow(value, (npx, part, cols))
            if step:
                mid_to_lines(other, my).start()
            else:
                pltpu.make_async_copy(mid.at[my], lines.at[:, rows_of(my), :], lines_come).start()
        loads[4].wait()
        whole(lines, lines_come).wait()
        half = npx // pairs
        for at in range(pairs):
            first = half * lax.rem(me // half + 1 + at, pairs)
            value = jnp.dot(
                ix[pl.ds(first, half)].reshape(half * rows, order_x),
                lines[...].reshape(order_x, cols),
                preferred_element_type=jnp.float32,
            )
            fin[pl.ds(first, half)] = narrow(value, (half, rows, cols))
            for other in (first, first + 1):
                @pl.when(other != me)
                def _():
                    fin_to(other).start()

                @pl.when(other == me)
                def _():
                    pltpu.make_async_copy(fin.at[me], out.at[me], out_recv.at[me]).start()

    for halo in halos_x + halos_y:
        halo.wait_send()

    def sent(other):
        whole(rhs.at[other], rhs_send.at[other]).wait()

        @pl.when(lax.rem(other, 2) == 0)
        def _():
            whole(fix_send.at[other], fix_sent.at[other]).wait()

        @pl.when(lax.rem(other, 2) == 1)
        def _():
            whole(fix_recv.at[:, 0], fix_sent.at[other]).wait()

    over_px(sent)
    for step in range(1, npy):
        other = lax.rem(my + step, npy)
        whole(mid.at[other], mid_send.at[other]).wait()

    @pl.when(x_first)
    def _():
        for step in range(1, npy):
            other = lax.rem(my + step, npy)
            whole(two.at[other], two_send.at[other]).wait()
        over_px(lambda other: whole(two.at[my, other], two_own.at[other]).wait())

    @pl.when(jnp.logical_not(x_first))
    def _():
        for step in range(1, npy):
            other = lax.rem(my + step, npy)
            whole(rhs.at[me, rows_of(other), :], own_send.at[other]).wait()
            whole(fix_send.at[me], fix_own.at[other]).wait()
        over_px(lambda other: whole(fin.at[other], fin_send.at[other]).wait())

    def settle(level, _):
        whole(out.at[level], out_recv.at[level]).wait()
        return 0

    lax.fori_loop(0, levels, settle, 0)


def fused(velocity, forcing, cross_x, cross_y, inv_x, inv_y):
    npx, npy = lax.axis_size("px"), lax.axis_size("py")
    levels, rows, cols = velocity.shape
    part = rows // npy
    shape, narrow = velocity.shape, jnp.bfloat16
    order_x, order_y = npx * rows, npy * cols
    vmem, dma = pltpu.VMEM, pltpu.SemaphoreType.DMA
    settled = pl.pallas_call(
        functools.partial(kernel, npx, npy),
        out_shape=jax.ShapeDtypeStruct(shape, narrow),
        in_specs=[pl.BlockSpec(memory_space=pl.ANY)] * 6,
        out_specs=pl.BlockSpec(memory_space=pl.ANY),
        scratch_shapes=[
            vmem(shape, jnp.float32),
            vmem(shape, narrow),
            vmem(shape, narrow),
            vmem(shape, narrow),
            vmem((npx, rows, order_x), narrow),
            vmem((order_y, order_y), narrow),
            vmem((2, levels, cols), jnp.float32),
            vmem((2, levels, cols), jnp.float32),
            vmem((2, levels, cols), jnp.float32),
            vmem((2, levels, rows), jnp.float32),
            vmem((2, levels, rows), jnp.float32),
            vmem((levels + 2, rows, cols), jnp.float32),
            vmem((levels + 2, rows, cols), jnp.float32),
            vmem(shape, jnp.float32),
            vmem((levels, rows, cols), narrow),
            vmem((npx, rows, cols), narrow),
            vmem((npx, part, order_y), narrow),
            vmem((npy, npx, part, cols), narrow),
            vmem((npy, npx, part, cols), narrow),
            vmem((npx, rows, cols), narrow),
            vmem((levels, 2, rows), jnp.float32),
            vmem((npy, npx, 2, rows), jnp.float32),
            vmem((128, rows), jnp.float32),
            vmem((rows, 128), jnp.float32),
            dma((6,)),
            dma((4,)),
            dma((4,)),
            dma((levels,)),
            dma((npy,)),
            dma((levels,)),
            dma((npy,)),
            dma,
            dma,
            dma,
            dma((npy,)),
            dma((npy,)),
            dma((npx,)),
            dma((npx,)),
            dma((levels,)),
        ],
        compiler_params=pltpu.CompilerParams(collective_id=0, has_side_effects=True, vmem_limit_bytes=56_000_000),
        cost_estimate=pl.CostEstimate(flops=4 * order_x * order_y * rows, bytes_accessed=8 * 1024 * 1024, transcendentals=0),
    )(
        velocity,
        forcing,
        cross_x,
        cross_y,
        inv_x.reshape(npx, rows, order_x),
        inv_y.reshape(order_y, order_y),
    )
    return velocity + settled.astype(jnp.float32)


def step(velocity, forcing, cross_x, cross_y, inv_x, inv_y):
    npx, npy = lax.axis_size("px"), lax.axis_size("py")
    levels, rows, cols = velocity.shape
    aligned = rows % (32 * npy) == 0 and rows % 128 == 0 and cols % 128 == 0 and levels % 8 == 0
    paired = npx % 2 == 0 and npy > 1 and 2 * npx * npy <= 128
    if aligned and paired and levels == npx and inv_x.shape[0] == 1:
        return fused(velocity, forcing, cross_x, cross_y, inv_x, inv_y)
    return shards(velocity, forcing, cross_x, cross_y, inv_x, inv_y)


def solution(mesh):
    return jax.shard_map(
        step,
        mesh=mesh,
        in_specs=(
            P(None, "px", "py"),
            P(None, "px", "py"),
            P(None, "px", "py"),
            P(None, "px", "py"),
            P("px", None, None),
            P("px", None, None),
        ),
        out_specs=P(None, "px", "py"),
        check_vma=False,
    )
```

time: 43.4 us -> 40.7 us (0.938)
  Pallas kernels: 42.2 us -> 39.5 us
    pallas_call x1, Pallas kernels: 42.2 us -> 39.5 us  [fused(): pl.pallas_call(functools.partial(kernel, npx, npy), out_shape=jax.ShapeDt...]
where the time goes in v1:
time: 40.7 us; the launch traced here: 40.6 us
  Pallas kernels  39.5 us (97%)
  other arithmetic  1.09 us (3%)
    pallas_call x1, Pallas kernels, fused(): pl.pallas_call(functools.partial(kernel, npx, npy), out_shape=jax.ShapeDt...  39.5 us
    add x1, other arithmetic, fused(): return velocity + settled.astype(jnp.float32)  1.09 us

profile of v1, /device:TPU:0, one launch (start us, length us, event | category | flops | bytes accessed | tf_op | source)
XLA Modules:
  0.0 40.6 jit_solution(380367377866229294)
XLA Ops:
  0.0 0.0 copy-start
  0.0 39.5 %shard_map.64 = bf16[8,128,256]{2,1,0:T(8,128)(2,1)S(1)} custom-call(f32[8,128,256]{2,1,0:T(8,128)} %vel_hbm.1, bf16[8,128,256]{2,1,0:T(8,128)(2,1)} %frc_hbm.1, bf16[8,128,256]{2,1,0:T(8,128)(2,1)} %cx_hbm.1, bf16[8,128,256]{2,1,0:T(8,128)(2,1)} %cy_hbm.1, bf16[8,128,1024]{2,1,0:T(8,128)(2,1)} %bitcast.2, bf16[1024,1024]{1,0:T(8,128)(2,1)} %bitcast.3), custom_call_target="tpu_custom_call" | custom-call | flops 536870912 | bytes 8388608 | tf_op jit(solution)/shard_map/pallas_call | solution.py:531
  39.5 0.0 copy-done
  39.5 1.1 %convert_add_fusion = f32[8,128,256]{2,1,0:T(8,128)} fusion(f32[8,128,256]{2,1,0:T(8,128)S(1)} %copy-done, bf16[8,128,256]{2,1,0:T(8,128)(2,1)S(1)} %shard_map.64), kind=kLoop, calls=%fused_computation | loop fusion | flops 524288 | bytes 2621440 | tf_op jit(solution)/shard_map/add | solution.py:587
Async XLA Ops:
  0.0 39.5 %copy-start = (f32[8,128,256]{2,1,0:T(8,128)S(1)}, f32[8,128,256]{2,1,0:T(8,128)}, u32[]{:S(2)}) copy-start(f32[8,128,256]{2,1,0:T(8,128)} %vel_hbm.1) | copy-start | bytes 3145732

commit v2 on v1

--- a/solution.py
+++ b/solution.py
@@ -101,14 +101,13 @@
     iy,
     x_send,
     x_recv,
-    x_mixed,
+    cx_ends,
     y_send,
     y_recv,
-    slope_x,
-    slope_y,
-    lap,
+    cy_ends,
     rhs,
     lines,
+    relay,
     cross,
     mid,
     two,
@@ -123,10 +122,12 @@
     rhs_send,
     own_send,
     fix_sent,
-    fix_own,
     fix_come,
     lines_come,
+    relay_come,
     cross_come,
+    pass_send,
+    ready,
     mid_send,
     two_send,
     two_own,
@@ -141,40 +142,35 @@
     x_first = lax.rem(me, 2) == 0
     pieces = [(vel_hbm, vel), (frc_hbm, frc), (cx_hbm, cx), (cy_hbm, cy), (ix_hbm, ix), (iy_hbm, iy)]
     loads = [pltpu.make_async_copy(a, b, load_sem.at[i]) for i, (a, b) in enumerate(pieces)]
-    loads[0].start()
+    for load in loads:
+        load.start()
 
     barrier = pltpu.get_barrier_semaphore()
 
-    def greet(at, _):
-        other = lax.rem(me * npy + my + at, npx * npy)
-        pl.semaphore_signal(
-            barrier, inc=1, device_id={"px": other // npy, "py": lax.rem(other, npy)}, device_id_type=pl.DeviceIdType.MESH
-        )
-        return 0
-
-    lax.fori_loop(1, npx * npy, greet, 0)
+    def greet(where):
+        pl.semaphore_signal(barrier, inc=1, device_id=where, device_id_type=pl.DeviceIdType.MESH)
+
+    twin = me + 1 - 2 * lax.rem(me, 2)
+    for step in range(1, npy):
+        other = lax.rem(my + step, npy)
+        greet({"py": other})
+        greet({"px": twin, "py": other})
+    for step in range(1, npx):
+        greet({"px": lax.rem(me + step, npx)})
     fix_rows[...] = jnp.zeros_like(fix_rows)
     loads[0].wait()
-    for load in loads[1:]:
-        load.start()
     lane = lax.broadcasted_iota(jnp.int32, (rows, 128), 1)
     zero = jnp.zeros((rows, 128), jnp.float32)
 
-    def ends_of(ref):
-        def one_level(level, faces):
-            first, last = faces
-            first = jnp.where(lane == level, ref[level, :, 0:1].astype(jnp.float32), first)
-            last = jnp.where(lane == level, ref[level, :, cols - 1 : cols].astype(jnp.float32), last)
-            return first, last
-
-        first, last = lax.fori_loop(0, levels, one_level, (zero, zero))
-        return jnp.transpose(first)[:levels], jnp.transpose(last)[:levels]
-
-    y_send[0], y_send[1] = ends_of(vel)
     for level in range(levels):
         x_send[0, level : level + 1, :] = vel[level, 0:1, :]
         x_send[1, level : level + 1, :] = vel[level, rows - 1 : rows, :]
-    pl.semaphore_wait(barrier, npx * npy - 1)
+    first, last = zero, zero
+    for level in range(levels):
+        first = jnp.where(lane == level, vel[level, :, 0:1], first)
+        last = jnp.where(lane == level, vel[level, :, cols - 1 : cols], last)
+    y_send[0], y_send[1] = jnp.transpose(first)[:levels], jnp.transpose(last)[:levels]
+    pl.semaphore_wait(barrier, npx - 1 + 2 * (npy - 1))
 
     up_x, down_x = lax.rem(me + 1, npx), lax.rem(me + npx - 1, npx)
     up_y, down_y = lax.rem(my + 1, npy), lax.rem(my + npy - 1, npy)
@@ -188,25 +184,10 @@
     ]
     for halo in halos_y + halos_x:
         halo.start()
-    row_at = lax.broadcasted_iota(jnp.int32, (rows, cols), 0)
-    col_at = lax.broadcasted_iota(jnp.int32, (rows, cols), 1)
-    blank = jnp.zeros((rows, cols), jnp.float32)
-    for edge in (0, levels + 1):
-        slope_x[edge] = blank
-        slope_y[edge] = blank
-
-    def slopes(level, _):
-        now = vel[level]
-        x_minus = jnp.where(row_at == 0, 0.0, pltpu.roll(now, 1, 0))
-        x_plus = jnp.where(row_at == rows - 1, 0.0, pltpu.roll(now, rows - 1, 0))
-        y_minus = jnp.where(col_at == 0, 0.0, pltpu.roll(now, 1, 1))
-        y_plus = jnp.where(col_at == cols - 1, 0.0, pltpu.roll(now, cols - 1, 1))
-        slope_x[level + 1] = 0.5 * (x_plus - x_minus)
-        slope_y[level + 1] = 0.5 * (y_plus - y_minus)
-        lap[level] = x_plus + x_minus + y_plus + y_minus - 4.0 * now
-        return 0
-
-    lax.fori_loop(0, levels, slopes, 0)
+    for step in range(2, npy - 1):
+        pl.semaphore_signal(
+            ready, inc=1, device_id={"py": lax.rem(my + step, npy)}, device_id_type=pl.DeviceIdType.MESH
+        )
     for load in loads[1:4]:
         load.wait()
 
@@ -217,15 +198,14 @@
         return pl.ds(pl.multiple_of(at * part, part), part)
 
     def inner(level):
-        above = jnp.minimum(level + 1, levels - 1)
-        below = jnp.maximum(level - 1, 0)
-        z_plus = jnp.where(level < levels - 1, 1.0, 0.0) * vel[above]
-        z_minus = jnp.where(level > 0, 1.0, 0.0) * vel[below]
-        total = lap[level] + z_plus + z_minus - 2.0 * vel[level]
-        total += cx[level].astype(jnp.float32) * (0.5 * (slope_x[level + 2] - slope_x[level]))
-        total += cy[level].astype(jnp.float32) * (0.5 * (slope_y[level + 2] - slope_y[level]))
-        total += frc[level].astype(jnp.float32)
-        lap[level] = total
+        now = vel[level]
+        above = jnp.where(level < levels - 1, 1.0, 0.0) * vel[jnp.minimum(level + 1, levels - 1)]
+        below = jnp.where(level > 0, 1.0, 0.0) * vel[jnp.maximum(level - 1, 0)]
+        rise = above - below
+        total = pltpu.roll(now, 1, 0) + pltpu.roll(now, rows - 1, 0) + pltpu.roll(now, 1, 1) + pltpu.roll(now, cols - 1, 1)
+        total += above + below - 6.0 * now + frc[level].astype(jnp.float32)
+        total += cx[level].astype(jnp.float32) * (0.25 * (pltpu.roll(rise, rows - 1, 0) - pltpu.roll(rise, 1, 0)))
+        total += cy[level].astype(jnp.float32) * (0.25 * (pltpu.roll(rise, cols - 1, 1) - pltpu.roll(rise, 1, 1)))
         rhs[level] = (time_step * total).astype(jnp.bfloat16)
 
     def to_cross(level, other):
@@ -246,6 +226,20 @@
         def _():
             pltpu.make_async_copy(src, dst, cross_come).start()
 
+    def to_relay(at, level, other):
+        send(
+            rhs.at[level, rows_of(other), :],
+            relay.at[lax.rem(me, 2), my, at],
+            rhs_send.at[level],
+            relay_come.at[lax.rem(me, 2), my, at],
+            {"px": 2 * (me // 2) + 1, "py": other},
+        ).start()
+
+    turn = jnp.where(my < npy // 2, 1, npy - 1)
+
+    def mate(step):
+        return lax.rem(my + step * turn, npy)
+
     def to_lines(level):
         @pl.when(level != me)
         def _():
@@ -260,108 +254,115 @@
     def level_of(at, odd):
         return 2 * lax.rem(me // 2 + 1 + at, pairs) + odd
 
-    def early(at, _):
-        level = level_of(at, 1)
-        inner(level)
-        for other in range(1, npy - 1):
-            to_cross(level, other)
+    here = level_of(pairs - 1, 1)
+
+    def one_pair(at, _):
+        odd = level_of(at, 1)
+        inner(odd)
+        for step in range(npy - 1, 0, -1):
+            to_relay(at, odd, mate(step))
+        even = level_of(at, 0)
+        inner(even)
+        to_lines(even)
         return 0
 
-    def early_even(at, _):
-        inner(level_of(at, 0))
+    def near_odd(at, _):
+        to_cross(level_of(at, 1), my)
         return 0
 
-    lax.fori_loop(0, pairs, early, 0)
-    lax.fori_loop(0, pairs, early_even, 0)
-    for halo in halos_x:
-        halo.wait_recv()
-
+    lax.fori_loop(0, pairs - 1, one_pair, 0)
+    inner(here)
+    for step in range(npy - 1, -1, -1):
+        to_cross(here, mate(step))
+    inner(here - 1)
+    to_lines(here - 1)
+    lax.fori_loop(0, pairs - 1, near_odd, 0)
     def level_slope(face):
         at = lax.broadcasted_iota(jnp.int32, face.shape, 0)
         lower = jnp.where(at == 0, 0.0, pltpu.roll(face, 1, 0))
         upper = jnp.where(at == levels - 1, 0.0, pltpu.roll(face, levels - 1, 0))
         return 0.25 * (upper - lower)
 
-    x_mixed[0] = -level_slope(x_recv[0])
-    x_mixed[1] = level_slope(x_recv[1])
-    slab_at = lax.broadcasted_iota(jnp.int32, (16, cols), 0)
-
-    def fix_x(level):
-        for end, first in enumerate((0, rows - 16)):
-            slab = slice(first, first + 16)
-            face = x_recv[end, pl.ds(level, 1), :] + cx[level, slab, :].astype(jnp.float32) * x_mixed[end, pl.ds(level, 1), :]
-            total = lap[level, slab, :] + jnp.where(slab_at == 15 * end, face, 0.0)
-            lap[level, slab, :] = total
-            rhs[level, slab, :] = (time_step * total).astype(jnp.bfloat16)
-
-    def late(at, _):
-        level = level_of(at, 1)
-        fix_x(level)
-        for other in sorted({0, npy - 1}):
-            to_cross(level, other)
-        return 0
-
-    def late_even(at, _):
-        level = level_of(at, 0)
-        fix_x(level)
-        to_lines(level)
-        return 0
-
-    lax.fori_loop(0, pairs, late, 0)
-    lax.fori_loop(0, pairs, late_even, 0)
-
-    near, far = ends_of(lap), ends_of(cy)
+    pick_row = lax.broadcasted_iota(jnp.int32, (16, cols), 0)
+    pick_col = lax.broadcasted_iota(jnp.int32, (16, cols), 1)
+    pick = ((pick_row == 0) & (pick_col == 0)) | ((pick_row == 1) & (pick_col == cols - 1))
+    picked = lax.dot_general(
+        pick.astype(jnp.bfloat16), cy[...].reshape(levels * rows, cols), (((1,), (1,)), ((), ())), preferred_element_type=jnp.float32
+    )
+    for end in range(2):
+        for level in range(levels):
+            cy_ends[end, level : level + 1, :] = picked[end : end + 1, level * rows : (level + 1) * rows]
+    for level in range(levels):
+        cx_ends[0, level : level + 1, :] = cx[level, 0:16, :].astype(jnp.float32)[0:1]
+        cx_ends[1, level : level + 1, :] = cx[level, rows - 16 : rows, :].astype(jnp.float32)[15:16]
+
+    def correct(end, came, gone, metric, lanes):
+        face = came[end] - gone[1 - end]
+        mixed = level_slope(face) if end else -level_slope(face)
+        value = time_step * (face + metric[end] * mixed)
+        for level in range(levels):
+            fix_send[level, end : end + 1, lanes] = value[level : level + 1, :]
+
+    for halo in halos_x:
+        halo.wait_recv()
+    for end in range(2):
+        correct(end, x_recv, x_send, cx_ends, slice(rows, rows + cols))
     for halo in halos_y:
         halo.wait_recv()
     for end in range(2):
-        face = y_recv[end]
-        mixed = level_slope(face) if end else -level_slope(face)
-        value = time_step * (near[end] + face + far[end] * mixed)
-        for level in range(levels):
-            fix_send[level, end : end + 1, :] = value[level : level + 1, :]
-
-    def fix_to(level, other, sem):
-        return send(fix_send.at[level], fix_recv.at[my, me], sem, fix_come, {"px": level, "py": other})
+        correct(end, y_recv, y_send, cy_ends, slice(0, rows))
+    if npy > 3:
+        pl.semaphore_wait(ready, npy - 3)
+
+    def fix_to(level, other, sem, lanes):
+        return send(
+            fix_send.at[level, :, pl.ds(0, lanes)],
+            fix_recv.at[my, me, :, pl.ds(0, lanes)],
+            sem,
+            fix_come,
+            {"px": level, "py": other},
+        )
+
+    def fix_here(level, lanes):
+        pltpu.make_async_copy(
+            fix_send.at[level, :, pl.ds(0, lanes)], fix_recv.at[my, me, :, pl.ds(0, lanes)], fix_come
+        ).start()
 
     def give_even(at, _):
         level = level_of(at, 0)
 
         @pl.when(level != me)
         def _():
-            fix_to(level, my, fix_sent.at[level]).start()
+            fix_to(level, my, fix_sent.at[level, my], rows + cols).start()
 
         @pl.when(level == me)
         def _():
-            pltpu.make_async_copy(fix_send.at[level], fix_recv.at[my, me], fix_come).start()
+            fix_here(level, rows + cols)
 
         return 0
+
+    def fix_lanes(other):
+        return rows + cols if other in (0, npy - 1) else rows
 
     def give_odd(at, _):
         level = level_of(at, 1)
         for other in range(npy):
-            @pl.when(level != me)
+            mine = (level == me) & (other == my)
+
+            @pl.when(jnp.logical_not(mine))
             def _():
-                fix_to(level, other, fix_sent.at[level]).start()
-
-            @pl.when((level == me) & (other != my))
+                fix_to(level, other, fix_sent.at[level, other], fix_lanes(other)).start()
+
+            @pl.when(mine)
             def _():
-                fix_to(level, other, fix_own.at[other]).start()
-
-            @pl.when((level == me) & (other == my))
-            def _():
-                pltpu.make_async_copy(fix_send.at[level], fix_recv.at[my, me], fix_come).start()
+                fix_here(level, fix_lanes(other))
 
         return 0
 
     lax.fori_loop(0, pairs, give_even, 0)
     lax.fori_loop(0, pairs, give_odd, 0)
 
-    order = [*range(1, npy), 0]
-    turn = jnp.where(my < npy // 2, 1, npy - 1)
-
-    def mate(step):
-        return lax.rem(my + step * turn, npy)
-
+    order = [*range(npy - 1, 0, -1), 0]
     def whole(ref, sem):
         return pltpu.make_async_copy(ref, ref, sem)
 
@@ -373,13 +374,29 @@
             first = where_cols + (cols - 128) * end
             now = ref[at, :, first : first + 128].astype(jnp.float32)
             spot = lane[: now.shape[0]] == 127 * end
-            ref[at, :, first : first + 128] = jnp.where(spot, value(end), now).astype(jnp.bfloat16)
+            ref[at, :, first : first + 128] = (now + jnp.where(spot, value(end), 0.0)).astype(jnp.bfloat16)
+
+    def mend_row(ref, at, first, end, where_cols, value):
+        spot = lax.broadcasted_iota(jnp.int32, (16, cols), 0) == 15 * end
+        block = (at, slice(first, first + 16), slice(where_cols, where_cols + cols))
+        ref[block] = (ref[block].astype(jnp.float32) + jnp.where(spot, value, 0.0)).astype(jnp.bfloat16)
 
     def mid_to_cross(other, source):
         return send(mid.at[other], cross.at[:, :, strip(source)], mid_send.at[other], cross_come, {"py": other})
 
     def mid_to_lines(other, source):
         return send(mid.at[other], lines.at[:, rows_of(source), :], mid_send.at[other], lines_come, {"py": other})
+
+    def pass_on(at, core, source):
+        spot = (core, source, at)
+        whole(relay.at[spot], relay_come.at[spot]).wait()
+        send(
+            relay.at[spot],
+            cross.at[2 * (me // 2) + core, :, strip(source)],
+            pass_send.at[core, source],
+            cross_come,
+            {"px": level_of(at, 1)},
+        ).start()
 
     def two_to(other_y, other_x, sem):
         return send(
@@ -398,13 +415,15 @@
 
     @pl.when(x_first)
     def _():
+        whole(lines, lines_come).wait()
         whole(fix_recv.at[my], fix_come).wait()
         for p in range(npx):
-            fix_rows[2 * p : 2 * p + 2, :] = fix_recv[my, p]
+            fix_rows[2 * p : 2 * p + 2, :] = fix_recv[my, p, :, 0:rows]
         fix_cols[...] = jnp.transpose(fix_rows[...])
-        whole(lines, lines_come).wait()
         for p in range(npx):
             mend(lines, p, 0, lambda end: fix_cols[:, 2 * p + end : 2 * p + end + 1])
+            for end in range(2):
+                mend_row(lines, p, (rows - 16) * end, end, 0, fix_recv[my, p, end : end + 1, rows : rows + cols])
         loads[4].wait()
         for step in order:
             other = mate(step)
@@ -435,17 +454,41 @@
 
     @pl.when(jnp.logical_not(x_first))
     def _():
-        whole(fix_recv, fix_come).wait()
+        def pass_level(at, _):
+            for step in range(1, npy):
+                for core in range(2):
+                    pass_on(at, core, mate(step))
+            return 0
+
+        lax.fori_loop(0, pairs - 1, pass_level, 0)
+        whole(cross, cross_come).wait()
+        outer = (my == 0) | (my == npy - 1)
+
+        @pl.when(outer)
+        def _():
+            whole(fix_recv, fix_come).wait()
+
+        @pl.when(jnp.logical_not(outer))
+        def _():
+            whole(fix_recv.at[:, :, :, pl.ds(0, rows)], fix_come).wait()
+
         for q in range(npy):
             for p in range(npx):
                 at = 2 * (q * npx + p)
-                fix_rows[at : at + 2, :] = fix_recv[q, p]
+                fix_rows[at : at + 2, :] = fix_recv[q, p, :, 0:rows]
         fix_cols[...] = jnp.transpose(fix_rows[...])
-        whole(cross, cross_come).wait()
         for q in range(npy):
             for p in range(npx):
                 at = 2 * (q * npx + p)
                 mend(cross, p, q * cols, lambda end: fix_cols[rows_of(my), at + end : at + end + 1])
+        for end in range(2):
+            @pl.when(my == (npy - 1) * end)
+            def _():
+                for q in range(npy):
+                    for p in range(npx):
+                        value = fix_recv[q, p, end : end + 1, rows : rows + cols]
+                        mend_row(cross, p, (part - 16) * end, end, q * cols, value)
+
         loads[5].wait()
         for step in order:
             other = mate(step)
@@ -488,11 +531,12 @@
 
         @pl.when(lax.rem(other, 2) == 0)
         def _():
-            whole(fix_send.at[other], fix_sent.at[other]).wait()
+            fix_to(other, my, fix_sent.at[other, my], rows + cols).wait_send()
 
         @pl.when(lax.rem(other, 2) == 1)
         def _():
-            whole(fix_recv.at[:, 0], fix_sent.at[other]).wait()
+            for plane in range(npy):
+                fix_to(other, plane, fix_sent.at[other, plane], fix_lanes(plane)).wait_send()
 
     over_px(sent)
     for step in range(1, npy):
@@ -511,7 +555,13 @@
         for step in range(1, npy):
             other = lax.rem(my + step, npy)
             whole(rhs.at[me, rows_of(other), :], own_send.at[other]).wait()
-            whole(fix_send.at[me], fix_own.at[other]).wait()
+            for core in range(2):
+                whole(relay.at[core, other], pass_send.at[core, other]).wait()
+        for plane in range(npy):
+            @pl.when(plane != my)
+            def _():
+                fix_to(me, plane, fix_sent.at[me, plane], fix_lanes(plane)).wait_send()
+
         over_px(lambda other: whole(fin.at[other], fin_send.at[other]).wait())
 
     def settle(level, _):
@@ -545,17 +595,16 @@
             vmem((2, levels, cols), jnp.float32),
             vmem((2, levels, rows), jnp.float32),
             vmem((2, levels, rows), jnp.float32),
-            vmem((levels + 2, rows, cols), jnp.float32),
-            vmem((levels + 2, rows, cols), jnp.float32),
-            vmem(shape, jnp.float32),
+            vmem((2, levels, rows), jnp.float32),
             vmem((levels, rows, cols), narrow),
             vmem((npx, rows, cols), narrow),
+            vmem((2, npy, max(npx // 2 - 1, 1), part, cols), narrow),
             vmem((npx, part, order_y), narrow),
             vmem((npy, npx, part, cols), narrow),
             vmem((npy, npx, part, cols), narrow),
             vmem((npx, rows, cols), narrow),
-            vmem((levels, 2, rows), jnp.float32),
-            vmem((npy, npx, 2, rows), jnp.float32),
+            vmem((levels, 2, rows + cols), jnp.float32),
+            vmem((npy, npx, 2, rows + cols), jnp.float32),
             vmem((128, rows), jnp.float32),
             vmem((rows, 128), jnp.float32),
             dma((6,)),
@@ -563,11 +612,13 @@
             dma((4,)),
             dma((levels,)),
             dma((npy,)),
-            dma((levels,)),
-            dma((npy,)),
+            dma((levels, npy)),
             dma,
             dma,
+            dma((2, npy, max(npx // 2 - 1, 1))),
             dma,
+            dma((2, npy)),
+            pltpu.SemaphoreType.REGULAR,
             dma((npy,)),
             dma((npy,)),
             dma((npx,)),
@@ -591,7 +642,7 @@
     npx, npy = lax.axis_size("px"), lax.axis_size("py")
     levels, rows, cols = velocity.shape
     aligned = rows % (32 * npy) == 0 and rows % 128 == 0 and cols % 128 == 0 and levels % 8 == 0
-    paired = npx % 2 == 0 and npy > 1 and 2 * npx * npy <= 128
+    paired = npx % 2 == 0 and npx > 2 and npy > 1 and 2 * npx * npy <= 128
     if aligned and paired and levels == npx and inv_x.shape[0] == 1:
         return fused(velocity, forcing, cross_x, cross_y, inv_x, inv_y)
     return shards(velocity, forcing, cross_x, cross_y, inv_x, inv_y)

time: 40.7 us -> 37.1 us (0.912)
  Pallas kernels: 39.5 us -> 35.8 us
    pallas_call x1, Pallas kernels: 39.5 us -> 35.8 us  [fused(): pl.pallas_call(functools.partial(kernel, npx, npy), out_shape=jax.ShapeDt...]
where the time goes in v2:
time: 37.1 us; the launch traced here: 36.9 us
  Pallas kernels  35.8 us (96%)
  other arithmetic  1.09 us (3%)
    pallas_call x1, Pallas kernels, fused(): pl.pallas_call(functools.partial(kernel, npx, npy), out_shape=jax.ShapeDt...  35.8 us
    add x1, other arithmetic, fused(): return velocity + settled.astype(jnp.float32)  1.09 us

profile of v2, /device:TPU:0, one launch (start us, length us, event | category | flops | bytes accessed | tf_op | source)
XLA Modules:
  0.0 36.9 jit_solution(7681090804138156694)
XLA Ops:
  0.0 0.0 copy-start
  0.0 35.8 %shard_map.64 = bf16[8,128,256]{2,1,0:T(8,128)(2,1)S(1)} custom-call(f32[8,128,256]{2,1,0:T(8,128)} %vel_hbm.1, bf16[8,128,256]{2,1,0:T(8,128)(2,1)} %frc_hbm.1, bf16[8,128,256]{2,1,0:T(8,128)(2,1)} %cx_hbm.1, bf16[8,128,256]{2,1,0:T(8,128)(2,1)} %cy_hbm.1, bf16[8,128,1024]{2,1,0:T(8,128)(2,1)} %bitcast.2, bf16[1024,1024]{1,0:T(8,128)(2,1)} %bitcast.3), custom_call_target="tpu_custom_call" | custom-call | flops 536870912 | bytes 8388608 | tf_op jit(solution)/shard_map/pallas_call | solution.py:581
  35.8 0.0 copy-done
  35.8 1.1 %convert_add_fusion = f32[8,128,256]{2,1,0:T(8,128)} fusion(f32[8,128,256]{2,1,0:T(8,128)S(1)} %copy-done, bf16[8,128,256]{2,1,0:T(8,128)(2,1)S(1)} %shard_map.64), kind=kLoop, calls=%fused_computation | loop fusion | flops 524288 | bytes 2621440 | tf_op jit(solution)/shard_map/add | solution.py:638
Async XLA Ops:
  0.0 35.8 %copy-start = (f32[8,128,256]{2,1,0:T(8,128)S(1)}, f32[8,128,256]{2,1,0:T(8,128)}, u32[]{:S(2)}) copy-start(f32[8,128,256]{2,1,0:T(8,128)} %vel_hbm.1) | copy-start | bytes 3145732

commit v3 on v2

--- a/solution.py
+++ b/solution.py
@@ -117,22 +117,23 @@
     fix_rows,
     fix_cols,
     load_sem,
-    halo_send,
-    halo_recv,
+    relay_come,
+    x_sent,
+    x_come,
+    y_sent,
+    y_come,
     rhs_send,
     own_send,
     fix_sent,
     fix_come,
     lines_come,
-    relay_come,
     cross_come,
     pass_send,
+    mid_send,
+    last_send,
+    out_recv,
     ready,
-    mid_send,
-    two_send,
-    two_own,
-    fin_send,
-    out_recv,
+    gate,
 ):
     me = lax.axis_index("px")
     my = lax.axis_index("py")
@@ -145,6 +146,9 @@
     for load in loads:
         load.start()
 
+    def whole(ref, sem):
+        return pltpu.make_async_copy(ref, ref, sem)
+
     barrier = pltpu.get_barrier_semaphore()
 
     def greet(where):
@@ -175,12 +179,12 @@
     up_x, down_x = lax.rem(me + 1, npx), lax.rem(me + npx - 1, npx)
     up_y, down_y = lax.rem(my + 1, npy), lax.rem(my + npy - 1, npy)
     halos_y = [
-        send(y_send.at[1], y_recv.at[0], halo_send.at[0], halo_recv.at[0], {"py": up_y}),
-        send(y_send.at[0], y_recv.at[1], halo_send.at[1], halo_recv.at[1], {"py": down_y}),
+        send(y_send.at[1], y_recv.at[0], y_sent, y_come, {"py": up_y}),
+        send(y_send.at[0], y_recv.at[1], y_sent, y_come, {"py": down_y}),
     ]
     halos_x = [
-        send(x_send.at[1], x_recv.at[0], halo_send.at[2], halo_recv.at[2], {"px": up_x}),
-        send(x_send.at[0], x_recv.at[1], halo_send.at[3], halo_recv.at[3], {"px": down_x}),
+        send(x_send.at[1], x_recv.at[0], x_sent, x_come, {"px": up_x}),
+        send(x_send.at[0], x_recv.at[1], x_sent, x_come, {"px": down_x}),
     ]
     for halo in halos_y + halos_x:
         halo.start()
@@ -216,22 +220,25 @@
 
         @pl.when(level != me)
         def _():
-            away(rhs_send.at[level]).start()
+            away(rhs_send).start()
 
         @pl.when((level == me) & (other != my))
         def _():
-            away(own_send.at[other]).start()
+            away(own_send).start()
 
         @pl.when((level == me) & (other == my))
         def _():
             pltpu.make_async_copy(src, dst, cross_come).start()
+
+    def gap(source, target):
+        return lax.rem(source - target + npy, npy) - 1
 
     def to_relay(at, level, other):
         send(
             rhs.at[level, rows_of(other), :],
-            relay.at[lax.rem(me, 2), my, at],
-            rhs_send.at[level],
-            relay_come.at[lax.rem(me, 2), my, at],
+            relay.at[at, gap(my, other), lax.rem(me, 2)],
+            rhs_send,
+            relay_come.at[at],
             {"px": 2 * (me // 2) + 1, "py": other},
         ).start()
 
@@ -243,7 +250,7 @@
     def to_lines(level):
         @pl.when(level != me)
         def _():
-            send(rhs.at[level], lines.at[me], rhs_send.at[level], lines_come, {"px": level}).start()
+            send(rhs.at[level], lines.at[me], rhs_send, lines_come, {"px": level}).start()
 
         @pl.when(level == me)
         def _():
@@ -303,12 +310,10 @@
         for level in range(levels):
             fix_send[level, end : end + 1, lanes] = value[level : level + 1, :]
 
-    for halo in halos_x:
-        halo.wait_recv()
+    whole(x_recv, x_come).wait()
     for end in range(2):
         correct(end, x_recv, x_send, cx_ends, slice(rows, rows + cols))
-    for halo in halos_y:
-        halo.wait_recv()
+    whole(y_recv, y_come).wait()
     for end in range(2):
         correct(end, y_recv, y_send, cy_ends, slice(0, rows))
     if npy > 3:
@@ -333,7 +338,7 @@
 
         @pl.when(level != me)
         def _():
-            fix_to(level, my, fix_sent.at[level, my], rows + cols).start()
+            fix_to(level, my, fix_sent, rows + cols).start()
 
         @pl.when(level == me)
         def _():
@@ -351,7 +356,7 @@
 
             @pl.when(jnp.logical_not(mine))
             def _():
-                fix_to(level, other, fix_sent.at[level, other], fix_lanes(other)).start()
+                fix_to(level, other, fix_sent, fix_lanes(other)).start()
 
             @pl.when(mine)
             def _():
@@ -362,10 +367,7 @@
     lax.fori_loop(0, pairs, give_even, 0)
     lax.fori_loop(0, pairs, give_odd, 0)
 
-    order = [*range(npy - 1, 0, -1), 0]
-    def whole(ref, sem):
-        return pltpu.make_async_copy(ref, ref, sem)
-
+    order = [*range(1, npy), 0]
     def narrow(value, shape):
         return value.astype(jnp.bfloat16).reshape(shape)
 
@@ -382,29 +384,27 @@
         ref[block] = (ref[block].astype(jnp.float32) + jnp.where(spot, value, 0.0)).astype(jnp.bfloat16)
 
     def mid_to_cross(other, source):
-        return send(mid.at[other], cross.at[:, :, strip(source)], mid_send.at[other], cross_come, {"py": other})
+        return send(mid.at[other], cross.at[:, :, strip(source)], mid_send, cross_come, {"py": other})
 
     def mid_to_lines(other, source):
-        return send(mid.at[other], lines.at[:, rows_of(source), :], mid_send.at[other], lines_come, {"py": other})
+        return send(mid.at[other], lines.at[:, rows_of(source), :], mid_send, lines_come, {"py": other})
 
     def pass_on(at, core, source):
-        spot = (core, source, at)
-        whole(relay.at[spot], relay_come.at[spot]).wait()
         send(
-            relay.at[spot],
+            relay.at[at, gap(source, my), core],
             cross.at[2 * (me // 2) + core, :, strip(source)],
-            pass_send.at[core, source],
+            pass_send,
             cross_come,
             {"px": level_of(at, 1)},
         ).start()
 
     def two_to(other_y, other_x, sem):
         return send(
-            two.at[other_y, other_x], out.at[me, rows_of(my), :], sem, out_recv.at[me], {"px": other_x, "py": other_y}
+            two.at[other_y * npx + other_x], out.at[me, rows_of(my), :], sem, out_recv, {"px": other_x, "py": other_y}
         )
 
     def fin_to(other):
-        return send(fin.at[other], out.at[me], fin_send.at[other], out_recv.at[me], {"px": other})
+        return send(fin.at[other], out.at[me], last_send, out_recv, {"px": other})
 
     def over_px(body):
         def one_step(at, _):
@@ -434,9 +434,10 @@
                 mid_to_cross(other, my).start()
             else:
                 pltpu.make_async_copy(mid.at[my], cross.at[:, :, strip(my)], cross_come).start()
+        whole(mid.at[pl.ds(0, npy - 1)], mid_send).wait()
         loads[5].wait()
         whole(cross, cross_come).wait()
-        for step in order:
+        for step in (0, *order[:-1]):
             other = mate(step)
             value = lax.dot_general(
                 cross[...].reshape(npx * part, order_y),
@@ -444,24 +445,26 @@
                 (((1,), (1,)), ((), ())),
                 preferred_element_type=jnp.float32,
             )
-            two[other] = narrow(value, (npx, part, cols))
-            if step:
-                over_px(lambda other_x: two_to(other, other_x, two_send.at[other]).start())
-                two_to(other, me, two_send.at[other]).start()
-            else:
-                over_px(lambda other_x: two_to(my, other_x, two_own.at[other_x]).start())
-                pltpu.make_async_copy(two.at[my, me], out.at[me, rows_of(my), :], out_recv.at[me]).start()
+            two[pl.ds(other * npx, npx)] = narrow(value, (npx, part, cols))
+            if not step:
+                over_px(lambda other_x: two_to(my, other_x, last_send).start())
+                pltpu.make_async_copy(two.at[my * npx + me], out.at[me, rows_of(my), :], out_recv).start()
+        pl.semaphore_wait(gate, 1)
+        for step in range(npy - 1, 0, -1):
+            other = mate(step)
+            over_px(lambda other_x: two_to(other, other_x, last_send).start())
+            two_to(other, me, last_send).start()
 
     @pl.when(jnp.logical_not(x_first))
     def _():
         def pass_level(at, _):
+            whole(relay.at[at], relay_come.at[at]).wait()
             for step in range(1, npy):
                 for core in range(2):
                     pass_on(at, core, mate(step))
             return 0
 
         lax.fori_loop(0, pairs - 1, pass_level, 0)
-        whole(cross, cross_come).wait()
         outer = (my == 0) | (my == npy - 1)
 
         @pl.when(outer)
@@ -477,6 +480,7 @@
                 at = 2 * (q * npx + p)
                 fix_rows[at : at + 2, :] = fix_recv[q, p, :, 0:rows]
         fix_cols[...] = jnp.transpose(fix_rows[...])
+        whole(cross, cross_come).wait()
         for q in range(npy):
             for p in range(npx):
                 at = 2 * (q * npx + p)
@@ -499,10 +503,11 @@
                 preferred_element_type=jnp.float32,
             )
             mid[other] = narrow(value, (npx, part, cols))
-            if step:
-                mid_to_lines(other, my).start()
-            else:
-                pltpu.make_async_copy(mid.at[my], lines.at[:, rows_of(my), :], lines_come).start()
+        pltpu.make_async_copy(mid.at[my], lines.at[:, rows_of(my), :], lines_come).start()
+        for step in range(npy - 1, 0, -1):
+            mid_to_lines(mate(step), my).start()
+        whole(mid.at[pl.ds(0, npy - 1)], mid_send).wait()
+        pl.semaphore_signal(gate, inc=1, device_id={"px": twin}, device_id_type=pl.DeviceIdType.MESH)
         loads[4].wait()
         whole(lines, lines_come).wait()
         half = npx // pairs
@@ -521,54 +526,38 @@
 
                 @pl.when(other == me)
                 def _():
-                    pltpu.make_async_copy(fin.at[me], out.at[me], out_recv.at[me]).start()
-
-    for halo in halos_x + halos_y:
-        halo.wait_send()
-
-    def sent(other):
-        whole(rhs.at[other], rhs_send.at[other]).wait()
-
-        @pl.when(lax.rem(other, 2) == 0)
-        def _():
-            fix_to(other, my, fix_sent.at[other, my], rows + cols).wait_send()
-
-        @pl.when(lax.rem(other, 2) == 1)
-        def _():
-            for plane in range(npy):
-                fix_to(other, plane, fix_sent.at[other, plane], fix_lanes(plane)).wait_send()
-
-    over_px(sent)
-    for step in range(1, npy):
-        other = lax.rem(my + step, npy)
-        whole(mid.at[other], mid_send.at[other]).wait()
+                    pltpu.make_async_copy(fin.at[me], out.at[me], out_recv).start()
+
+    whole(x_send, x_sent).wait()
+    whole(y_send, y_sent).wait()
+
+    whole(rhs.at[pl.ds(0, levels - 1)], rhs_send).wait()
+
+    def fix_done(level, _):
+        @pl.when((level != me) & (lax.rem(level, 2) == 0))
+        def _():
+            fix_to(level, my, fix_sent, rows + cols).wait_send()
+
+        for plane in range(npy):
+            @pl.when((lax.rem(level, 2) == 1) & ((level != me) | (plane != my)))
+            def _():
+                fix_to(level, plane, fix_sent, fix_lanes(plane)).wait_send()
+
+        return 0
+
+    lax.fori_loop(0, levels, fix_done, 0)
 
     @pl.when(x_first)
     def _():
-        for step in range(1, npy):
-            other = lax.rem(my + step, npy)
-            whole(two.at[other], two_send.at[other]).wait()
-        over_px(lambda other: whole(two.at[my, other], two_own.at[other]).wait())
+        whole(two.at[pl.ds(0, npy * npx - 1)], last_send).wait()
 
     @pl.when(jnp.logical_not(x_first))
     def _():
-        for step in range(1, npy):
-            other = lax.rem(my + step, npy)
-            whole(rhs.at[me, rows_of(other), :], own_send.at[other]).wait()
-            for core in range(2):
-                whole(relay.at[core, other], pass_send.at[core, other]).wait()
-        for plane in range(npy):
-            @pl.when(plane != my)
-            def _():
-                fix_to(me, plane, fix_sent.at[me, plane], fix_lanes(plane)).wait_send()
-
-        over_px(lambda other: whole(fin.at[other], fin_send.at[other]).wait())
-
-    def settle(level, _):
-        whole(out.at[level], out_recv.at[level]).wait()
-        return 0
-
-    lax.fori_loop(0, levels, settle, 0)
+        whole(rhs.at[me, pl.ds(0, rows - part)], own_send).wait()
+        whole(relay, pass_send).wait()
+        whole(fin.at[pl.ds(0, npx - 1)], last_send).wait()
+
+    whole(out, out_recv).wait()
 
 
 def fused(velocity, forcing, cross_x, cross_y, inv_x, inv_y):
@@ -598,32 +587,19 @@
             vmem((2, levels, rows), jnp.float32),
             vmem((levels, rows, cols), narrow),
             vmem((npx, rows, cols), narrow),
-            vmem((2, npy, max(npx // 2 - 1, 1), part, cols), narrow),
+            vmem((npx // 2 - 1, npy - 1, 2, part, cols), narrow),
             vmem((npx, part, order_y), narrow),
             vmem((npy, npx, part, cols), narrow),
-            vmem((npy, npx, part, cols), narrow),
+            vmem((npy * npx, part, cols), narrow),
             vmem((npx, rows, cols), narrow),
             vmem((levels, 2, rows + cols), jnp.float32),
             vmem((npy, npx, 2, rows + cols), jnp.float32),
             vmem((128, rows), jnp.float32),
             vmem((rows, 128), jnp.float32),
             dma((6,)),
-            dma((4,)),
-            dma((4,)),
-            dma((levels,)),
-            dma((npy,)),
-            dma((levels, npy)),
-            dma,
-            dma,
-            dma((2, npy, max(npx // 2 - 1, 1))),
-            dma,
-            dma((2, npy)),
-            pltpu.SemaphoreType.REGULAR,
-            dma((npy,)),
-            dma((npy,)),
-            dma((npx,)),
-            dma((npx,)),
-            dma((levels,)),
+            dma((npx // 2 - 1,)),
+            *[dma] * 14,
+            *[pltpu.SemaphoreType.REGULAR] * 2,
         ],
         compiler_params=pltpu.CompilerParams(collective_id=0, has_side_effects=True, vmem_limit_bytes=56_000_000),
         cost_estimate=pl.CostEstimate(flops=4 * order_x * order_y * rows, bytes_accessed=8 * 1024 * 1024, transcendentals=0),

time: 37.1 us -> 34 us (0.916)
  Pallas kernels: 35.8 us -> 32.8 us
    pallas_call x1, Pallas kernels: 35.8 us -> 32.8 us  [fused(): pl.pallas_call(functools.partial(kernel, npx, npy), out_shape=jax.ShapeDt...]
where the time goes in v3:
time: 34 us; the launch traced here: 33.9 us
  Pallas kernels  32.8 us (96%)
  other arithmetic  1.09 us (3%)
    pallas_call x1, Pallas kernels, fused(): pl.pallas_call(functools.partial(kernel, npx, npy), out_shape=jax.ShapeDt...  32.8 us
    add x1, other arithmetic, fused(): return velocity + settled.astype(jnp.float32)  1.09 us

profile of v3, /device:TPU:0, one launch (start us, length us, event | category | flops | bytes accessed | tf_op | source)
XLA Modules:
  0.0 33.9 jit_solution(4385875818797461398)
XLA Ops:
  0.0 0.0 copy-start
  0.0 32.8 %shard_map.64 = bf16[8,128,256]{2,1,0:T(8,128)(2,1)S(1)} custom-call(f32[8,128,256]{2,1,0:T(8,128)} %vel_hbm.1, bf16[8,128,256]{2,1,0:T(8,128)(2,1)} %frc_hbm.1, bf16[8,128,256]{2,1,0:T(8,128)(2,1)} %cx_hbm.1, bf16[8,128,256]{2,1,0:T(8,128)(2,1)} %cy_hbm.1, bf16[8,128,1024]{2,1,0:T(8,128)(2,1)} %bitcast.2, bf16[1024,1024]{1,0:T(8,128)(2,1)} %bitcast.3), custom_call_target="tpu_custom_call" | custom-call | flops 536870912 | bytes 8388608 | tf_op jit(solution)/shard_map/pallas_call | solution.py:570
  32.8 0.0 copy-done
  32.8 1.1 %convert_add_fusion = f32[8,128,256]{2,1,0:T(8,128)} fusion(f32[8,128,256]{2,1,0:T(8,128)S(1)} %copy-done, bf16[8,128,256]{2,1,0:T(8,128)(2,1)S(1)} %shard_map.64), kind=kLoop, calls=%fused_computation | loop fusion | flops 524288 | bytes 2621440 | tf_op jit(solution)/shard_map/add | solution.py:614
Async XLA Ops:
  0.0 32.8 %copy-start = (f32[8,128,256]{2,1,0:T(8,128)S(1)}, f32[8,128,256]{2,1,0:T(8,128)}, u32[]{:S(2)}) copy-start(f32[8,128,256]{2,1,0:T(8,128)} %vel_hbm.1) | copy-start | bytes 3145732

commit v4 on v3

--- a/solution.py
+++ b/solution.py
@@ -114,8 +114,10 @@
     fin,
     fix_send,
     fix_recv,
-    fix_rows,
-    fix_cols,
+    row_recv,
+    spread,
+    delta,
+    extra,
     load_sem,
     relay_come,
     x_sent,
@@ -126,6 +128,7 @@
     own_send,
     fix_sent,
     fix_come,
+    row_come,
     lines_come,
     cross_come,
     pass_send,
@@ -161,7 +164,8 @@
         greet({"px": twin, "py": other})
     for step in range(1, npx):
         greet({"px": lax.rem(me + step, npx)})
-    fix_rows[...] = jnp.zeros_like(fix_rows)
+    spread[...] = jnp.zeros_like(spread)
+    delta[...] = jnp.zeros_like(delta)
     loads[0].wait()
     lane = lax.broadcasted_iota(jnp.int32, (rows, 128), 1)
     zero = jnp.zeros((rows, 128), jnp.float32)
@@ -278,12 +282,9 @@
         return 0
 
     lax.fori_loop(0, pairs - 1, one_pair, 0)
-    inner(here)
-    for step in range(npy - 1, -1, -1):
-        to_cross(here, mate(step))
     inner(here - 1)
     to_lines(here - 1)
-    lax.fori_loop(0, pairs - 1, near_odd, 0)
+    inner(here)
     def level_slope(face):
         at = lax.broadcasted_iota(jnp.int32, face.shape, 0)
         lower = jnp.where(at == 0, 0.0, pltpu.roll(face, 1, 0))
@@ -310,9 +311,26 @@
         for level in range(levels):
             fix_send[level, end : end + 1, lanes] = value[level : level + 1, :]
 
+    def row_to(level):
+        return send(fix_send.at[level, :, pl.ds(rows, cols)], row_recv.at[me], fix_sent, row_come, {"px": level})
+
+    def give_row(at, _):
+        level = level_of(at, 0)
+
+        @pl.when(level != me)
+        def _():
+            row_to(level).start()
+
+        @pl.when(level == me)
+        def _():
+            pltpu.make_async_copy(fix_send.at[level, :, pl.ds(rows, cols)], row_recv.at[me], row_come).start()
+
+        return 0
+
     whole(x_recv, x_come).wait()
     for end in range(2):
         correct(end, x_recv, x_send, cx_ends, slice(rows, rows + cols))
+    lax.fori_loop(0, pairs, give_row, 0)
     whole(y_recv, y_come).wait()
     for end in range(2):
         correct(end, y_recv, y_send, cy_ends, slice(0, rows))
@@ -333,54 +351,68 @@
             fix_send.at[level, :, pl.ds(0, lanes)], fix_recv.at[my, me, :, pl.ds(0, lanes)], fix_come
         ).start()
 
-    def give_even(at, _):
-        level = level_of(at, 0)
-
-        @pl.when(level != me)
-        def _():
-            fix_to(level, my, fix_sent, rows + cols).start()
-
-        @pl.when(level == me)
-        def _():
-            fix_here(level, rows + cols)
-
-        return 0
-
-    def fix_lanes(other):
-        return rows + cols if other in (0, npy - 1) else rows
-
-    def give_odd(at, _):
-        level = level_of(at, 1)
+    def fix_lanes(other, odd):
+        return rows + cols if odd and other in (0, npy - 1) else rows
+
+    def give(at, odd):
+        level = level_of(at, odd)
         for other in range(npy):
             mine = (level == me) & (other == my)
 
             @pl.when(jnp.logical_not(mine))
             def _():
-                fix_to(level, other, fix_sent, fix_lanes(other)).start()
+                fix_to(level, other, fix_sent, fix_lanes(other, odd)).start()
 
             @pl.when(mine)
             def _():
-                fix_here(level, fix_lanes(other))
+                fix_here(level, fix_lanes(other, odd))
 
         return 0
 
-    lax.fori_loop(0, pairs, give_even, 0)
-    lax.fori_loop(0, pairs, give_odd, 0)
+    lax.fori_loop(0, pairs, lambda at, _: give(at, 0), 0)
+    lax.fori_loop(0, pairs, lambda at, _: give(at, 1), 0)
+    for step in range(npy - 1, -1, -1):
+        to_cross(here, mate(step))
+    lax.fori_loop(0, pairs - 1, near_odd, 0)
 
     order = [*range(1, npy), 0]
     def narrow(value, shape):
         return value.astype(jnp.bfloat16).reshape(shape)
 
-    def mend(ref, at, where_cols, value):
-        for end in range(2):
-            first = where_cols + (cols - 128) * end
-            now = ref[at, :, first : first + 128].astype(jnp.float32)
-            spot = lane[: now.shape[0]] == 127 * end
-            ref[at, :, first : first + 128] = (now + jnp.where(spot, value(end), 0.0)).astype(jnp.bfloat16)
+    def prepare(matrix):
+        for q in range(npy):
+            for p in range(npx):
+                spread[2 * q : 2 * q + 2, p * rows : (p + 1) * rows] = fix_recv[q, p, :, 0:rows]
+        moved = lax.dot_general(
+            spread[...].astype(jnp.bfloat16), matrix, (((1,), (1,)), ((), ())), preferred_element_type=jnp.float32
+        )
+        spare = jnp.zeros((128 - moved.shape[0], moved.shape[1]), jnp.float32)
+        moved = jnp.transpose(jnp.concatenate([moved, spare], axis=0))
+        spot = lax.broadcasted_iota(jnp.int32, moved.shape, 1)
+        for q in range(npy):
+            for end in range(2):
+                tile = slice(q * cols + (cols - 128) * end, q * cols + (cols - 128) * end + 128)
+                column = moved[:, 2 * q + end : 2 * q + end + 1]
+                now = delta[:, tile].astype(jnp.float32)
+                delta[:, tile] = (now + jnp.where(spot == 127 * end, column, 0.0)).astype(jnp.bfloat16)
+
+    def across(ref, other):
+        return lax.dot_general(
+            ref, iy[strip(other), :], (((1,), (1,)), ((), ())), preferred_element_type=jnp.float32
+        )
+
+    def prepare_extra():
+        loads[5].wait()
+
+        def one(q, _):
+            extra[q] = across(delta[...], q)
+            return 0
+
+        lax.fori_loop(0, npy, one, 0)
 
     def mend_row(ref, at, first, end, where_cols, value):
         spot = lax.broadcasted_iota(jnp.int32, (16, cols), 0) == 15 * end
-        block = (at, slice(first, first + 16), slice(where_cols, where_cols + cols))
+        block = (*at, slice(first, first + 16), slice(where_cols, where_cols + cols))
         ref[block] = (ref[block].astype(jnp.float32) + jnp.where(spot, value, 0.0)).astype(jnp.bfloat16)
 
     def mid_to_cross(other, source):
@@ -406,6 +438,13 @@
     def fin_to(other):
         return send(fin.at[other], out.at[me], last_send, out_recv, {"px": other})
 
+    def away_px(body):
+        def one_step(at, _):
+            body(lax.rem(2 * (me // 2) + at, npx))
+            return 0
+
+        lax.fori_loop(2, npx, one_step, 0)
+
     def over_px(body):
         def one_step(at, _):
             body(lax.rem(me + at, npx))
@@ -416,14 +455,10 @@
     @pl.when(x_first)
     def _():
         whole(lines, lines_come).wait()
-        whole(fix_recv.at[my], fix_come).wait()
+        whole(row_recv, row_come).wait()
         for p in range(npx):
-            fix_rows[2 * p : 2 * p + 2, :] = fix_recv[my, p, :, 0:rows]
-        fix_cols[...] = jnp.transpose(fix_rows[...])
-        for p in range(npx):
-            mend(lines, p, 0, lambda end: fix_cols[:, 2 * p + end : 2 * p + end + 1])
             for end in range(2):
-                mend_row(lines, p, (rows - 16) * end, end, 0, fix_recv[my, p, end : end + 1, rows : rows + cols])
+                mend_row(lines, (p,), (rows - 16) * end, end, 0, row_recv[p, end : end + 1, :])
         loads[4].wait()
         for step in order:
             other = mate(step)
@@ -434,17 +469,14 @@
                 mid_to_cross(other, my).start()
             else:
                 pltpu.make_async_copy(mid.at[my], cross.at[:, :, strip(my)], cross_come).start()
+        whole(fix_recv.at[:, :, :, pl.ds(0, rows)], fix_come).wait()
+        prepare(ix[:, rows_of(my), :].reshape(npx * part, order_x))
+        prepare_extra()
         whole(mid.at[pl.ds(0, npy - 1)], mid_send).wait()
-        loads[5].wait()
         whole(cross, cross_come).wait()
         for step in (0, *order[:-1]):
             other = mate(step)
-            value = lax.dot_general(
-                cross[...].reshape(npx * part, order_y),
-                iy[strip(other), :],
-                (((1,), (1,)), ((), ())),
-                preferred_element_type=jnp.float32,
-            )
+            value = across(cross[...].reshape(npx * part, order_y), other) + extra[other]
             two[pl.ds(other * npx, npx)] = narrow(value, (npx, part, cols))
             if not step:
                 over_px(lambda other_x: two_to(my, other_x, last_send).start())
@@ -452,8 +484,11 @@
         pl.semaphore_wait(gate, 1)
         for step in range(npy - 1, 0, -1):
             other = mate(step)
-            over_px(lambda other_x: two_to(other, other_x, last_send).start())
+            two_to(other, twin, last_send).start()
             two_to(other, me, last_send).start()
+        for step in range(npy - 1, 0, -1):
+            other = mate(step)
+            away_px(lambda other_x: two_to(other, other_x, last_send).start())
 
     @pl.when(jnp.logical_not(x_first))
     def _():
@@ -475,37 +510,26 @@
         def _():
             whole(fix_recv.at[:, :, :, pl.ds(0, rows)], fix_come).wait()
 
-        for q in range(npy):
-            for p in range(npx):
-                at = 2 * (q * npx + p)
-                fix_rows[at : at + 2, :] = fix_recv[q, p, :, 0:rows]
-        fix_cols[...] = jnp.transpose(fix_rows[...])
-        whole(cross, cross_come).wait()
-        for q in range(npy):
-            for p in range(npx):
-                at = 2 * (q * npx + p)
-                mend(cross, p, q * cols, lambda end: fix_cols[rows_of(my), at + end : at + end + 1])
+        line = lax.broadcasted_iota(jnp.int32, (npx * part, order_x), 0)
+        column = lax.broadcasted_iota(jnp.int32, (npx * part, order_x), 1)
+        prepare((column == line // part * rows + my * part + lax.rem(line, part)).astype(jnp.bfloat16))
         for end in range(2):
             @pl.when(my == (npy - 1) * end)
             def _():
                 for q in range(npy):
                     for p in range(npx):
                         value = fix_recv[q, p, end : end + 1, rows : rows + cols]
-                        mend_row(cross, p, (part - 16) * end, end, q * cols, value)
-
-        loads[5].wait()
-        for step in order:
+                        mend_row(delta, (), p * part + (part - 16) * end, end, q * cols, value)
+
+        prepare_extra()
+        whole(cross, cross_come).wait()
+        for step in (*range(npy - 1, 0, -1), 0):
             other = mate(step)
-            value = lax.dot_general(
-                cross[...].reshape(npx * part, order_y),
-                iy[strip(other), :],
-                (((1,), (1,)), ((), ())),
-                preferred_element_type=jnp.float32,
-            )
+            value = across(cross[...].reshape(npx * part, order_y), other) + extra[other]
             mid[other] = narrow(value, (npx, part, cols))
+            if step:
+                mid_to_lines(other, my).start()
         pltpu.make_async_copy(mid.at[my], lines.at[:, rows_of(my), :], lines_come).start()
-        for step in range(npy - 1, 0, -1):
-            mid_to_lines(mate(step), my).start()
         whole(mid.at[pl.ds(0, npy - 1)], mid_send).wait()
         pl.semaphore_signal(gate, inc=1, device_id={"px": twin}, device_id_type=pl.DeviceIdType.MESH)
         loads[4].wait()
@@ -534,14 +558,17 @@
     whole(rhs.at[pl.ds(0, levels - 1)], rhs_send).wait()
 
     def fix_done(level, _):
-        @pl.when((level != me) & (lax.rem(level, 2) == 0))
-        def _():
-            fix_to(level, my, fix_sent, rows + cols).wait_send()
-
-        for plane in range(npy):
-            @pl.when((lax.rem(level, 2) == 1) & ((level != me) | (plane != my)))
-            def _():
-                fix_to(level, plane, fix_sent, fix_lanes(plane)).wait_send()
+        odd = lax.rem(level, 2)
+
+        @pl.when((level != me) & (odd == 0))
+        def _():
+            row_to(level).wait_send()
+
+        for kind in range(2):
+            for plane in range(npy):
+                @pl.when((odd == kind) & ((level != me) | (plane != my)))
+                def _():
+                    fix_to(level, plane, fix_sent, fix_lanes(plane, kind)).wait_send()
 
         return 0
 
@@ -594,11 +621,13 @@
             vmem((npx, rows, cols), narrow),
             vmem((levels, 2, rows + cols), jnp.float32),
             vmem((npy, npx, 2, rows + cols), jnp.float32),
-            vmem((128, rows), jnp.float32),
-            vmem((rows, 128), jnp.float32),
+            vmem((npx, 2, cols), jnp.float32),
+            vmem((-(-2 * npy // 16) * 16, order_x), jnp.float32),
+            vmem((npx * part, order_y), narrow),
+            vmem((npy, npx * part, cols), jnp.float32),
             dma((6,)),
             dma((npx // 2 - 1,)),
-            *[dma] * 14,
+            *[dma] * 15,
             *[pltpu.SemaphoreType.REGULAR] * 2,
         ],
         compiler_params=pltpu.CompilerParams(collective_id=0, has_side_effects=True, vmem_limit_bytes=56_000_000),
@@ -618,7 +647,7 @@
     npx, npy = lax.axis_size("px"), lax.axis_size("py")
     levels, rows, cols = velocity.shape
     aligned = rows % (32 * npy) == 0 and rows % 128 == 0 and cols % 128 == 0 and levels % 8 == 0
-    paired = npx % 2 == 0 and npx > 2 and npy > 1 and 2 * npx * npy <= 128
+    paired = npx % 2 == 0 and npx > 2 and npy > 1 and 2 * npy <= 128
     if aligned and paired and levels == npx and inv_x.shape[0] == 1:
         return fused(velocity, forcing, cross_x, cross_y, inv_x, inv_y)
     return shards(velocity, forcing, cross_x, cross_y, inv_x, inv_y)

time: 34 us -> 33.8 us (level)
  the two profiles are of different devices: /device:TPU:0 before, /device:TPU:19 now
where the time goes in v4:
time: 33.8 us; the launch traced here: 33.6 us
  Pallas kernels  32.5 us (96%)
  other arithmetic  1.09 us (3%)
    pallas_call x1, Pallas kernels, fused(): pl.pallas_call(functools.partial(kernel, npx, npy), out_shape=jax.ShapeDt...  32.5 us
    add x1, other arithmetic, fused(): return velocity + settled.astype(jnp.float32)  1.09 us

profile of v4, /device:TPU:19, one launch (start us, length us, event | category | flops | bytes accessed | tf_op | source)
XLA Modules:
  0.0 33.6 jit_solution(3941883865225085762)
XLA Ops:
  0.0 0.0 copy-start
  0.0 32.5 %shard_map.64 = bf16[8,128,256]{2,1,0:T(8,128)(2,1)S(1)} custom-call(f32[8,128,256]{2,1,0:T(8,128)} %vel_hbm.1, bf16[8,128,256]{2,1,0:T(8,128)(2,1)} %frc_hbm.1, bf16[8,128,256]{2,1,0:T(8,128)(2,1)} %cx_hbm.1, bf16[8,128,256]{2,1,0:T(8,128)(2,1)} %cy_hbm.1, bf16[8,128,1024]{2,1,0:T(8,128)(2,1)} %bitcast.2, bf16[1024,1024]{1,0:T(8,128)(2,1)} %bitcast.3), custom_call_target="tpu_custom_call" | custom-call | flops 536870912 | bytes 8388608 | tf_op jit(solution)/shard_map/pallas_call | solution.py:597
  32.5 0.0 copy-done
  32.5 1.1 %convert_add_fusion = f32[8,128,256]{2,1,0:T(8,128)} fusion(f32[8,128,256]{2,1,0:T(8,128)S(1)} %copy-done, bf16[8,128,256]{2,1,0:T(8,128)(2,1)S(1)} %shard_map.64), kind=kLoop, calls=%fused_computation | loop fusion | flops 524288 | bytes 2621440 | tf_op jit(solution)/shard_map/add | solution.py:643
Async XLA Ops:
  0.0 32.5 %copy-start = (f32[8,128,256]{2,1,0:T(8,128)S(1)}, f32[8,128,256]{2,1,0:T(8,128)}, u32[]{:S(2)}) copy-start(f32[8,128,256]{2,1,0:T(8,128)} %vel_hbm.1) | copy-start | bytes 3145732

commit v5 on v4

--- a/solution.py
+++ b/solution.py
@@ -251,6 +251,13 @@
     def mate(step):
         return lax.rem(my + step * turn, npy)
 
+    outermost = (my == 0) | (my == npy - 1)
+    ahead = [*range(1, npy)]
+    swapped = [*ahead[1::-1], *ahead[2:]]
+
+    def peers(inner):
+        return [mate(jnp.where(outermost, *steps)) for steps in zip(ahead, inner)]
+
     def to_lines(level):
         @pl.when(level != me)
         def _():
@@ -460,8 +467,8 @@
             for end in range(2):
                 mend_row(lines, (p,), (rows - 16) * end, end, 0, row_recv[p, end : end + 1, :])
         loads[4].wait()
-        for step in order:
-            other = mate(step)
+        for other in (*peers(swapped), None):
+            step, other = other is not None, my if other is None else other
             mine = ix[:, rows_of(other), :].reshape(npx * part, order_x)
             value = jnp.dot(mine, lines[...].reshape(order_x, cols), preferred_element_type=jnp.float32)
             mid[other] = narrow(value, (npx, part, cols))
@@ -482,12 +489,10 @@
                 over_px(lambda other_x: two_to(my, other_x, last_send).start())
                 pltpu.make_async_copy(two.at[my * npx + me], out.at[me, rows_of(my), :], out_recv).start()
         pl.semaphore_wait(gate, 1)
-        for step in range(npy - 1, 0, -1):
-            other = mate(step)
+        for other in peers(ahead[::-1]):
             two_to(other, twin, last_send).start()
             two_to(other, me, last_send).start()
-        for step in range(npy - 1, 0, -1):
-            other = mate(step)
+        for other in peers(ahead[::-1]):
             away_px(lambda other_x: two_to(other, other_x, last_send).start())
 
     @pl.when(jnp.logical_not(x_first))
@@ -523,8 +528,8 @@
 
         prepare_extra()
         whole(cross, cross_come).wait()
-        for step in (*range(npy - 1, 0, -1), 0):
-            other = mate(step)
+        for other in (*peers(swapped), None):
+            step, other = other is not None, my if other is None else other
             value = across(cross[...].reshape(npx * part, order_y), other) + extra[other]
             mid[other] = narrow(value, (npx, part, cols))
             if step:

time: 33.8 us -> 32.9 us (0.973)
  the two profiles are of different devices: /device:TPU:19 before, /device:TPU:0 now
where the time goes in v5:
time: 32.9 us; the launch traced here: 32.8 us
  Pallas kernels  31.7 us (96%)
  other arithmetic  1.09 us (3%)
    pallas_call x1, Pallas kernels, fused(): pl.pallas_call(functools.partial(kernel, npx, npy), out_shape=jax.ShapeDt...  31.7 us
    add x1, other arithmetic, fused(): return velocity + settled.astype(jnp.float32)  1.09 us

profile of v5, /device:TPU:0, one launch (start us, length us, event | category | flops | bytes accessed | tf_op | source)
XLA Modules:
  0.0 32.8 jit_solution(14286222315438601589)
XLA Ops:
  0.0 0.0 copy-start
  0.0 31.7 %shard_map.64 = bf16[8,128,256]{2,1,0:T(8,128)(2,1)S(1)} custom-call(f32[8,128,256]{2,1,0:T(8,128)} %vel_hbm.1, bf16[8,128,256]{2,1,0:T(8,128)(2,1)} %frc_hbm.1, bf16[8,128,256]{2,1,0:T(8,128)(2,1)} %cx_hbm.1, bf16[8,128,256]{2,1,0:T(8,128)(2,1)} %cy_hbm.1, bf16[8,128,1024]{2,1,0:T(8,128)(2,1)} %bitcast.2, bf16[1024,1024]{1,0:T(8,128)(2,1)} %bitcast.3), custom_call_target="tpu_custom_call" | custom-call | flops 536870912 | bytes 8388608 | tf_op jit(solution)/shard_map/pallas_call | solution.py:602
  31.7 0.0 copy-done
  31.7 1.1 %convert_add_fusion = f32[8,128,256]{2,1,0:T(8,128)} fusion(f32[8,128,256]{2,1,0:T(8,128)S(1)} %copy-done, bf16[8,128,256]{2,1,0:T(8,128)(2,1)S(1)} %shard_map.64), kind=kLoop, calls=%fused_computation | loop fusion | flops 524288 | bytes 2621440 | tf_op jit(solution)/shard_map/add | solution.py:648
Async XLA Ops:
  0.0 31.7 %copy-start = (f32[8,128,256]{2,1,0:T(8,128)S(1)}, f32[8,128,256]{2,1,0:T(8,128)}, u32[]{:S(2)}) copy-start(f32[8,128,256]{2,1,0:T(8,128)} %vel_hbm.1) | copy-start | bytes 3145732

commit v6 on v5

--- a/solution.py
+++ b/solution.py
@@ -277,8 +277,8 @@
     def one_pair(at, _):
         odd = level_of(at, 1)
         inner(odd)
-        for step in range(npy - 1, 0, -1):
-            to_relay(at, odd, mate(step))
+        for other in peers(swapped):
+            to_relay(at, odd, other)
         even = level_of(at, 0)
         inner(even)
         to_lines(even)
@@ -488,12 +488,35 @@
             if not step:
                 over_px(lambda other_x: two_to(my, other_x, last_send).start())
                 pltpu.make_async_copy(two.at[my * npx + me], out.at[me, rows_of(my), :], out_recv).start()
-        pl.semaphore_wait(gate, 1)
-        for other in peers(ahead[::-1]):
+        first, *rest = peers(ahead[::-1])
+
+        def near_of(other):
             two_to(other, twin, last_send).start()
             two_to(other, me, last_send).start()
-        for other in peers(ahead[::-1]):
+
+        def away_of(other):
             away_px(lambda other_x: two_to(other, other_x, last_send).start())
+
+        @pl.when(jnp.logical_not(outermost))
+        def _():
+            near_of(first)
+            away_of(first)
+
+        pl.semaphore_wait(gate, 1)
+
+        @pl.when(outermost)
+        def _():
+            near_of(first)
+
+        for other in rest:
+            near_of(other)
+
+        @pl.when(outermost)
+        def _():
+            away_of(first)
+
+        for other in rest:
+            away_of(other)
 
     @pl.when(jnp.logical_not(x_first))
     def _():

time: 32.9 us -> 32.8 us (level)
  no operation moved by 1% of the time
where the time goes in v6:
time: 32.8 us; the launch traced here: 32.7 us
  Pallas kernels  31.6 us (96%)
  other arithmetic  1.09 us (3%)
    pallas_call x1, Pallas kernels, fused(): pl.pallas_call(functools.partial(kernel, npx, npy), out_shape=jax.ShapeDt...  31.6 us
    add x1, other arithmetic, fused(): return velocity + settled.astype(jnp.float32)  1.09 us

profile of v6, /device:TPU:0, one launch (start us, length us, event | category | flops | bytes accessed | tf_op | source)
XLA Modules:
  0.0 32.7 jit_solution(2028955081610630416)
XLA Ops:
  0.0 0.0 copy-start
  0.0 31.6 %shard_map.64 = bf16[8,128,256]{2,1,0:T(8,128)(2,1)S(1)} custom-call(f32[8,128,256]{2,1,0:T(8,128)} %vel_hbm.1, bf16[8,128,256]{2,1,0:T(8,128)(2,1)} %frc_hbm.1, bf16[8,128,256]{2,1,0:T(8,128)(2,1)} %cx_hbm.1, bf16[8,128,256]{2,1,0:T(8,128)(2,1)} %cy_hbm.1, bf16[8,128,1024]{2,1,0:T(8,128)(2,1)} %bitcast.2, bf16[1024,1024]{1,0:T(8,128)(2,1)} %bitcast.3), custom_call_target="tpu_custom_call" | custom-call | flops 536870912 | bytes 8388608 | tf_op jit(solution)/shard_map/pallas_call | solution.py:625
  31.6 0.0 copy-done
  31.6 1.1 %convert_add_fusion = f32[8,128,256]{2,1,0:T(8,128)} fusion(f32[8,128,256]{2,1,0:T(8,128)S(1)} %copy-done, bf16[8,128,256]{2,1,0:T(8,128)(2,1)S(1)} %shard_map.64), kind=kLoop, calls=%fused_computation | loop fusion | flops 524288 | bytes 2621440 | tf_op jit(solution)/shard_map/add | solution.py:671
Async XLA Ops:
  0.0 31.6 %copy-start = (f32[8,128,256]{2,1,0:T(8,128)S(1)}, f32[8,128,256]{2,1,0:T(8,128)}, u32[]{:S(2)}) copy-start(f32[8,128,256]{2,1,0:T(8,128)} %vel_hbm.1) | copy-start | bytes 3145732

commit v7 on v6

--- a/solution.py
+++ b/solution.py
@@ -242,7 +242,7 @@
             rhs.at[level, rows_of(other), :],
             relay.at[at, gap(my, other), lax.rem(me, 2)],
             rhs_send,
-            relay_come.at[at],
+            relay_come.at[at, gap(my, other)],
             {"px": 2 * (me // 2) + 1, "py": other},
         ).start()
 
@@ -521,8 +521,9 @@
     @pl.when(jnp.logical_not(x_first))
     def _():
         def pass_level(at, _):
-            whole(relay.at[at], relay_come.at[at]).wait()
             for step in range(1, npy):
+                spot = (at, gap(mate(step), my))
+                whole(relay.at[spot], relay_come.at[spot]).wait()
                 for core in range(2):
                     pass_on(at, core, mate(step))
             return 0
@@ -654,7 +655,7 @@
             vmem((npx * part, order_y), narrow),
             vmem((npy, npx * part, cols), jnp.float32),
             dma((6,)),
-            dma((npx // 2 - 1,)),
+            dma((npx // 2 - 1, npy - 1)),
             *[dma] * 15,
             *[pltpu.SemaphoreType.REGULAR] * 2,
         ],

time: 32.8 us -> 33.3 us (1.015)
  Pallas kernels: 31.6 us -> 32.1 us
    pallas_call x1, Pallas kernels: 31.6 us -> 32.1 us  [fused(): pl.pallas_call(functools.partial(kernel, npx, npy), out_shape=jax.ShapeDt...]
where the time goes in v7:
time: 33.3 us; the launch traced here: 33.2 us
  Pallas kernels  32.1 us (96%)
  other arithmetic  1.09 us (3%)
    pallas_call x1, Pallas kernels, fused(): pl.pallas_call(functools.partial(kernel, npx, npy), out_shape=jax.ShapeDt...  32.1 us
    add x1, other arithmetic, fused(): return velocity + settled.astype(jnp.float32)  1.09 us

profile of v7, /device:TPU:0, one launch (start us, length us, event | category | flops | bytes accessed | tf_op | source)
XLA Modules:
  0.0 33.2 jit_solution(13263089361987916352)
XLA Ops:
  0.0 0.0 copy-start
  0.0 32.1 %shard_map.64 = bf16[8,128,256]{2,1,0:T(8,128)(2,1)S(1)} custom-call(f32[8,128,256]{2,1,0:T(8,128)} %vel_hbm.1, bf16[8,128,256]{2,1,0:T(8,128)(2,1)} %frc_hbm.1, bf16[8,128,256]{2,1,0:T(8,128)(2,1)} %cx_hbm.1, bf16[8,128,256]{2,1,0:T(8,128)(2,1)} %cy_hbm.1, bf16[8,128,1024]{2,1,0:T(8,128)(2,1)} %bitcast.2, bf16[1024,1024]{1,0:T(8,128)(2,1)} %bitcast.3), custom_call_target="tpu_custom_call" | custom-call | flops 536870912 | bytes 8388608 | tf_op jit(solution)/shard_map/pallas_call | solution.py:626
  32.1 0.0 copy-done
  32.1 1.1 %convert_add_fusion = f32[8,128,256]{2,1,0:T(8,128)} fusion(f32[8,128,256]{2,1,0:T(8,128)S(1)} %copy-done, bf16[8,128,256]{2,1,0:T(8,128)(2,1)S(1)} %shard_map.64), kind=kLoop, calls=%fused_computation | loop fusion | flops 524288 | bytes 2621440 | tf_op jit(solution)/shard_map/add | solution.py:672
Async XLA Ops:
  0.0 32.1 %copy-start = (f32[8,128,256]{2,1,0:T(8,128)S(1)}, f32[8,128,256]{2,1,0:T(8,128)}, u32[]{:S(2)}) copy-start(f32[8,128,256]{2,1,0:T(8,128)} %vel_hbm.1) | copy-start | bytes 3145732
